TPU v7x, 128 devices: a whole 4x4x4 slice. The times are simulated.
128 devices in a mesh: seg: 2 (over core), dp: 64 (over z, y, x).
Axes of the slice: x: 4, y: 4, z: 4, core: 2. Of those that a mesh axis runs over, the one named last changes fastest.
Arguments:
- query_rows: bfloat16 [64, 1024, 1280], P('dp', 'seg'), may hold values from -160 to 160
- key_rows: bfloat16 [64, 1024, 1280], P('dp', 'seg'), may hold values from -8 to 8
- value_rows: bfloat16 [64, 1024, 1280], P('dp', 'seg'), may hold values from -6 to 6
- prompt_keys: bfloat16 [64, 100, 1280], P('dp', 'seg'), may hold values from -6 to 6
- prompt_values: bfloat16 [64, 100, 1280], P('dp', 'seg'), may hold values from -6 to 6
- out_grad: bfloat16 [64, 1024, 2560], P('dp', 'seg'), may hold values from -54 to 54
- w_out: bfloat16 [1280, 2560], replicated, may hold values from -0.15625 to 0.15625
Outputs:
- query_grad: bfloat16 [64, 1024, 1280], P('dp', 'seg')
- key_grad: bfloat16 [64, 1024, 1280], P('dp', 'seg')
- value_grad: bfloat16 [64, 1024, 1280], P('dp', 'seg')
- prompt_key_grad: bfloat16 [64, 100, 1280], P('dp', 'seg')
- prompt_value_grad: bfloat16 [64, 100, 1280], P('dp', 'seg')
- weight_grad: bfloat16 [1280, 2560], replicated
All inputs are finite; a program needn't handle non-finite values.
Results may differ from a plain program's by a relative error of at most 0.0058.
Values may be sent and summed in bfloat16 or wider, within the bound.
No kernel may reach another device: no remote copies, remote signals or barrier semaphores. Data moves between devices by JAX's collectives and lax.ppermute only.
A program may use at most 256 MiB of HBM per device.

v0:
```python
import functools
import math

import jax
import jax.numpy as jnp
from jax import lax
from jax.experimental import pallas as pl
from jax.experimental.pallas import tpu as pltpu
from jax.sharding import PartitionSpec as P


HEADS = 16
HD = 80
SUMS = 50
PAD = 64
TOK = 512
WIDTH = HEADS * HD
D = 2560
HALF = D // 2
QUAD = 4 * HD
WIN = 384
BLK = 256
SCALE = HD**-0.5
C2 = SCALE * math.log2(math.e)
NEG = -1e30
SIDE = 4
TILES = HALF // 128
SUB = QUAD // SIDE
PIECE = SUB * TILES
STAT = 8
ORDER = 6
BF = jnp.bfloat16
F32 = jnp.float32


def dot(a, b):
    return lax.dot_general(a, b, (((1,), (0,)), ((), ())), preferred_element_type=F32)


def dot_nt(a, b):
    return lax.dot_general(a, b, (((1,), (1,)), ((), ())), preferred_element_type=F32)


def iota(shape, dim):
    return lax.broadcasted_iota(jnp.int32, shape, dim)


def fwd_kernel(place, s_ref, q_hbm, k_hbm, v_hbm, pk_hbm, pv_hbm, *rest):
    o_ref, lse_ref, q_ref, k_ref, v_ref, pk_ref, pv_ref, vt_ref, pvt_ref, pk_in, pv_in, sem = rest[-12:]
    segment = s_ref[0]
    quad = s_ref[ORDER + place]
    odd = quad & 1
    window = pl.ds(pl.multiple_of(((quad * 5) >> 1) * 128, 128), WIN)
    pk_ref[...] = jnp.zeros_like(pk_ref)
    pv_ref[...] = jnp.zeros_like(pv_ref)
    moves = [
        pltpu.make_async_copy(src.at[:, window], dst, sem.at[n])
        for n, (src, dst) in enumerate(
            (
                (q_hbm, q_ref),
                (k_hbm, k_ref),
                (pk_hbm, pk_in),
                (v_hbm, v_ref),
                (pv_hbm, pv_in),
            )
        )
    ]
    for move in moves:
        move.start()
    for move in moves[:3]:
        move.wait()
    pk_ref[:SUMS] = pk_in[...]
    for move in moves[3:]:
        move.wait()
    pv_ref[:SUMS] = pv_in[...]
    vt_ref[...] = jnp.transpose(v_ref[...])
    pvt_ref[...] = jnp.transpose(pv_ref[...])
    lanes = iota((TOK, BLK), 1)
    causal = iota((BLK, BLK), 0) <= iota((BLK, BLK), 1)
    seen = iota((PAD, TOK), 0) < SUMS * segment

    def head(h, at):
        low = 64 * odd + HD * h - at
        w = pl.ds(at, BLK)
        mine = (lanes >= low) & (lanes < low + HD)
        qm = jnp.where(mine, q_ref[:, w], jnp.zeros((), BF))
        s0 = dot_nt(k_ref[:BLK, w], qm)
        s1 = dot_nt(k_ref[BLK:, w], qm[BLK:])
        sp = jnp.where(seen, dot_nt(pk_ref[:, w], qm), NEG)
        s00 = jnp.where(causal, s0[:, :BLK], NEG)
        s01 = s0[:, BLK:]
        s11 = jnp.where(causal, s1, NEG)
        mp = jnp.max(sp, 0, keepdims=True)
        m0 = jnp.maximum(jnp.max(s00, 0, keepdims=True), mp[:, :BLK])
        m1 = jnp.maximum(
            jnp.maximum(jnp.max(s01, 0, keepdims=True), jnp.max(s11, 0, keepdims=True)), mp[:, BLK:]
        )
        e00 = jnp.exp2((s00 - m0) * C2)
        e01 = jnp.exp2((s01 - m1) * C2)
        e11 = jnp.exp2((s11 - m1) * C2)
        ep0 = jnp.exp2((sp[:, :BLK] - m0) * C2)
        ep1 = jnp.exp2((sp[:, BLK:] - m1) * C2)
        l0 = jnp.sum(e00, 0, keepdims=True) + jnp.sum(ep0, 0, keepdims=True)
        l1 = (
            jnp.sum(e01, 0, keepdims=True)
            + jnp.sum(e11, 0, keepdims=True)
            + jnp.sum(ep1, 0, keepdims=True)
        )
        row = pl.ds(pl.multiple_of(64 * odd + HD * h, 16), HD)
        to = slice(HD * h, HD * h + HD)
        vt = vt_ref[row, :]
        pvt = pvt_ref[row, :]
        o0 = dot(vt[:, :BLK], e00.astype(BF)) + dot(pvt, ep0.astype(BF))
        o1 = (
            dot(vt[:, :BLK], e01.astype(BF))
            + dot(vt[:, BLK:], e11.astype(BF))
            + dot(pvt, ep1.astype(BF))
        )
        o_ref[to, :BLK] = (o0 / l0).astype(BF)
        o_ref[to, BLK:] = (o1 / l1).astype(BF)
        lse_ref[pl.ds(h, 1), :BLK] = m0 * C2 + jnp.log2(l0)
        lse_ref[pl.ds(h, 1), BLK:] = m1 * C2 + jnp.log2(l1)

    for h in range(4):
        head(h, h // 2 * 128)


def forward_quad(place, scalars, q, k, v, pk, pv, after):
    any_spec = pl.BlockSpec(memory_space=pl.ANY)
    return pl.pallas_call(
        functools.partial(fwd_kernel, place),
        out_shape=(
            jax.ShapeDtypeStruct((QUAD, TOK), BF),
            jax.ShapeDtypeStruct((4, TOK), F32),
        ),
        grid_spec=pltpu.PrefetchScalarGridSpec(
            num_scalar_prefetch=1,
            grid=(1,),
            in_specs=[any_spec] * (5 + len(after)),
            out_specs=(
                pl.BlockSpec((QUAD, TOK), lambda i, s: (0, 0)),
                pl.BlockSpec((4, TOK), lambda i, s: (0, 0)),
            ),
            scratch_shapes=[
                pltpu.VMEM((TOK, WIN), BF),
                pltpu.VMEM((TOK, WIN), BF),
                pltpu.VMEM((TOK, WIN), BF),
                pltpu.VMEM((PAD, WIN), BF),
                pltpu.VMEM((PAD, WIN), BF),
                pltpu.VMEM((WIN, TOK), BF),
                pltpu.VMEM((WIN, PAD), BF),
                pltpu.VMEM((SUMS, WIN), BF),
                pltpu.VMEM((SUMS, WIN), BF),
                pltpu.SemaphoreType.DMA((5,)),
            ],
        ),
        compiler_params=pltpu.CompilerParams(vmem_limit_bytes=24 << 20),
        cost_estimate=pl.CostEstimate(
            flops=4 * 2 * 2 * 896 * 256 * 256, transcendentals=4 * 896 * 256, bytes_accessed=1600000
        ),
        name="fwd_quad",
    )(scalars, q, k, v, pk, pv, *after)


def bwd_kernel(
    s_ref, q_ref, k_ref, v_ref, g_ref, pk_in, pv_in, lse_0, lse_1, lse_2, lse_3,
    dq_ref, dk_ref, dv_ref, dp_ref,
    kt_ref, pkt_ref, dqt_ref, dka_ref, dva_ref, dpka_ref, dpva_ref, pk_ref, pv_ref, lse_ref,
):
    for n in range(2):
        lse = lse_0[...]
        for place, other in ((1, lse_1), (2, lse_2), (3, lse_3)):
            lse = jnp.where(s_ref[ORDER + place] == 2 * pl.program_id(0) + n, other[...], lse)
        lse_ref[4 * n : 4 * n + 4] = lse
    segment = s_ref[0]
    pk_ref[...] = jnp.zeros_like(pk_ref)
    pv_ref[...] = jnp.zeros_like(pv_ref)
    pk_ref[:SUMS] = pk_in[...]
    pv_ref[:SUMS] = pv_in[...]
    kt_ref[...] = jnp.transpose(k_ref[...])
    pkt_ref[...] = jnp.transpose(pk_ref[...])
    for acc in (dka_ref, dva_ref, dpka_ref, dpva_ref):
        acc[...] = jnp.zeros_like(acc)
    causal = iota((BLK, BLK), 0) <= iota((BLK, BLK), 1)
    seen = iota((PAD, TOK), 0) < SUMS * segment
    for h in range(8):
        low = HD * h
        at = low // 128 * 128
        wide = 128 if low - at + HD <= 128 else 256
        w = slice(at, at + wide)
        lanes = iota((TOK, wide), 1) + at
        mine = (lanes >= low) & (lanes < low + HD)
        qm = jnp.where(mine, q_ref[:, w], jnp.zeros((), BF))
        gm = jnp.where(mine, g_ref[:, w], jnp.zeros((), BF))
        lse = lse_ref[h : h + 1, :]
        lse0, lse1 = lse[:, :BLK], lse[:, BLK:]
        s0 = dot_nt(k_ref[:BLK, w], qm)
        s1 = dot_nt(k_ref[BLK:, w], qm[BLK:])
        sp = dot_nt(pk_ref[:, w], qm)
        p00 = jnp.exp2(jnp.where(causal, s0[:, :BLK] * C2 - lse0, NEG))
        p01 = jnp.exp2(s0[:, BLK:] * C2 - lse1)
        p11 = jnp.exp2(jnp.where(causal, s1 * C2 - lse1, NEG))
        pp = jnp.exp2(jnp.where(seen, sp * C2 - lse, NEG))
        d0 = dot_nt(v_ref[:BLK, w], gm)
        d11 = dot_nt(v_ref[BLK:, w], gm[BLK:])
        dp = dot_nt(pv_ref[:, w], gm)
        d00, d01 = d0[:, :BLK], d0[:, BLK:]
        deltap = jnp.sum(pp * dp, 0, keepdims=True)
        delta0 = jnp.sum(p00 * d00, 0, keepdims=True) + deltap[:, :BLK]
        delta1 = (
            jnp.sum(p01 * d01, 0, keepdims=True)
            + jnp.sum(p11 * d11, 0, keepdims=True)
            + deltap[:, BLK:]
        )
        delta = jnp.concatenate([delta0, delta1], 1)
        t00 = (p00 * (d00 - delta0) * SCALE).astype(BF)
        t01 = (p01 * (d01 - delta1) * SCALE).astype(BF)
        t11 = (p11 * (d11 - delta1) * SCALE).astype(BF)
        tp = (pp * (dp - delta) * SCALE).astype(BF)
        t0 = jnp.concatenate([t00, t01], 1)
        row = slice(low, low + HD)
        dqt = dot(kt_ref[row, :BLK], t0) + dot(pkt_ref[row, :], tp)
        dqt_ref[row, :BLK] = dqt[:, :BLK].astype(BF)
        dqt_ref[row, BLK:] = (dqt[:, BLK:] + dot(kt_ref[row, BLK:], t11)).astype(BF)
        dka_ref[:BLK, w] += dot(t0, qm)
        dka_ref[BLK:, w] += dot(t11, qm[BLK:])
        dpka_ref[:, w] += dot(tp, qm)
        low0 = jnp.concatenate([p00.astype(BF), p01.astype(BF)], 1)
        dva_ref[:BLK, w] += dot(low0, gm)
        dva_ref[BLK:, w] += dot(p11.astype(BF), gm[BLK:])
        dpva_ref[:, w] += dot(pp.astype(BF), gm)
    dq_ref[...] = jnp.transpose(dqt_ref[...])
    dk_ref[...] = dka_ref[...].astype(BF)
    dv_ref[...] = dva_ref[...].astype(BF)
    dp_ref[0] = dpka_ref[:SUMS].astype(BF)
    dp_ref[1] = dpva_ref[:SUMS].astype(BF)


def backward(scalars, q, k, v, g, pk, pv, lses):
    wide = 8 * HD
    rows = pl.BlockSpec((TOK, wide), lambda i, s: (0, i))
    prompt = pl.BlockSpec((SUMS, wide), lambda i, s: (0, i))
    return pl.pallas_call(
        bwd_kernel,
        out_shape=(jax.ShapeDtypeStruct((TOK, WIDTH), BF),) * 3
        + (jax.ShapeDtypeStruct((2, SUMS, WIDTH), BF),),
        grid_spec=pltpu.PrefetchScalarGridSpec(
            num_scalar_prefetch=1,
            grid=(2,),
            in_specs=[rows] * 4 + [prompt] * 2 + [pl.BlockSpec((4, TOK), lambda i, s: (0, 0))] * 4,
            out_specs=(rows, rows, rows, pl.BlockSpec((2, SUMS, wide), lambda i, s: (0, 0, i))),
            scratch_shapes=[
                pltpu.VMEM((wide, TOK), BF),
                pltpu.VMEM((wide, PAD), BF),
                pltpu.VMEM((wide, TOK), BF),
                pltpu.VMEM((TOK, wide), F32),
                pltpu.VMEM((TOK, wide), F32),
                pltpu.VMEM((PAD, wide), F32),
                pltpu.VMEM((PAD, wide), F32),
                pltpu.VMEM((PAD, wide), BF),
                pltpu.VMEM((PAD, wide), BF),
                pltpu.VMEM((8, TOK), F32),
            ],
        ),
        compiler_params=pltpu.CompilerParams(vmem_limit_bytes=36 << 20),
        cost_estimate=pl.CostEstimate(
            flops=16 * 5 * 2 * 896 * 256 * 256, transcendentals=16 * 896 * 256, bytes_accessed=10000000
        ),
        name="attend_back",
    )(scalars, q, k, v, g, pk, pv, *lses)


WCOLS = 640


def weight_kernel(bys, places, s_ref, *refs):
    owns, others, g_ref, h_ref = refs[:places], refs[places : 2 * places], refs[2 * places], refs[2 * places + 1]
    outs, picked = refs[2 * places + 2 : -1], refs[-1]
    for n, by in enumerate(bys):
        quad = (s_ref[1] + by) & (SIDE - 1)
        for j in range(places):

            @pl.when((pl.program_id(0) == 0) & (quad == s_ref[ORDER + j]))
            def _():
                picked[n, 0] = owns[j][...]
                picked[n, 1] = others[j][...]

    for n, out_ref in enumerate(outs):
        out = dot(picked[n, 0], g_ref[...]) + dot(picked[n, 1], h_ref[...])
        for sub in range(SIDE):
            for tile in range(WCOLS // 128):
                out_ref[sub, tile] = out[sub * SUB : sub * SUB + SUB, tile * 128 : tile * 128 + 128].astype(
                    out_ref.dtype
                )


def weight_quads(bys, scalars, owns, others, grad_rows, grad_other):
    count, places = len(bys), len(owns)
    quad = pl.BlockSpec((QUAD, TOK), lambda n, s: (0, 0))
    columns = pl.BlockSpec((TOK, WCOLS), lambda n, s: (0, n + s[0] * (HALF // WCOLS)))
    outs = pl.pallas_call(
        functools.partial(weight_kernel, bys, places),
        out_shape=[jax.ShapeDtypeStruct((SIDE, TILES, SUB, 128), BF if by else F32) for by in bys],
        grid_spec=pltpu.PrefetchScalarGridSpec(
            num_scalar_prefetch=1,
            grid=(HALF // WCOLS,),
            in_specs=[quad] * (2 * places) + [columns, columns],
            out_specs=[pl.BlockSpec((SIDE, WCOLS // 128, SUB, 128), lambda n, s: (0, n, 0, 0))] * count,
            scratch_shapes=[pltpu.VMEM((count, 2, QUAD, TOK), BF)],
        ),
        compiler_params=pltpu.CompilerParams(vmem_limit_bytes=24 << 20),
        cost_estimate=pl.CostEstimate(
            flops=count * 4 * QUAD * TOK * HALF, transcendentals=0, bytes_accessed=4200000
        ),
        name="weight_quads",
    )(scalars, *owns, *others, grad_rows, grad_other)
    return [out.reshape(SIDE, PIECE, 128) for out in outs]


def order_kernel(s_ref, o_ref):
    segment, chip = s_ref[0], s_ref[1]
    x, y, z = chip & 3, (chip >> 2) & 3, chip >> 4
    p0 = (x + 2) & 3
    p1 = jnp.where(x == y, x + 1, y + 2) & 3
    p2 = (p0 + jnp.where(((p0 + 1) & 3) == p1, 2, 1)) & 3
    turn = jnp.where(segment == 0, x, y)
    sub = jnp.where(segment == 0, z, x)
    for n, value in enumerate((segment, turn, sub, x, y, z, p0, p1, p2, 6 - p0 - p1 - p2)):
        o_ref[n] = value


def order_scalars(where):
    smem = pl.BlockSpec(memory_space=pltpu.SMEM)
    return pl.pallas_call(
        order_kernel,
        out_shape=jax.ShapeDtypeStruct((ORDER + SIDE,), jnp.int32),
        in_specs=[smem],
        out_specs=smem,
        compiler_params=pltpu.CompilerParams(vmem_limit_bytes=1 << 20),
        cost_estimate=pl.CostEstimate(flops=6000000000, transcendentals=0, bytes_accessed=64),
        name="order",
    )(where)


def line_kernel(s_ref, own, r1, r2, r3, o0, o1, o2, o3):
    total = (own[0] + r2[0].astype(F32)) + (r1[0].astype(F32) + r3[0].astype(F32))
    for by, out in enumerate((o0, o1, o2, o3)):

        @pl.when(pl.program_id(0) == by)
        def _():
            out[...] = total.astype(out.dtype)


def sum_line(scalars, own, r1, r2, r3):
    block = pl.BlockSpec((1, PIECE, 128), lambda n, s: ((s[2] + n) % SIDE, 0, 0))
    whole = pl.BlockSpec((PIECE, 128), lambda n, s: (0, 0))
    return pl.pallas_call(
        line_kernel,
        out_shape=[jax.ShapeDtypeStruct((PIECE, 128), kind) for kind in (F32, BF, BF, BF)],
        grid_spec=pltpu.PrefetchScalarGridSpec(
            num_scalar_prefetch=1, grid=(SIDE,), in_specs=[block] * 4, out_specs=[whole] * 4
        ),
        compiler_params=pltpu.CompilerParams(vmem_limit_bytes=16 << 20),
        cost_estimate=pl.CostEstimate(flops=2000000, transcendentals=0, bytes_accessed=5000000),
        name="sum_line",
    )(scalars, own, r1, r2, r3)


def mid_kernel(own, r1, r2, r3, out):
    total = (own[...] + r2[...].astype(F32)) + (r1[...].astype(F32) + r3[...].astype(F32))
    out[...] = total.astype(BF)


def sum_mid(own, r1, r2, r3):
    return pl.pallas_call(
        mid_kernel,
        out_shape=jax.ShapeDtypeStruct((PIECE, 128), BF),
        compiler_params=pltpu.CompilerParams(vmem_limit_bytes=8 << 20),
        cost_estimate=pl.CostEstimate(flops=400000, transcendentals=0, bytes_accessed=1200000),
        name="sum_mid",
    )(own, r1, r2, r3)


def cross_kernel(own, r1, r2, r3, out):
    total = (own[...].astype(F32) + r2[...].astype(F32)) + (r1[...].astype(F32) + r3[...].astype(F32))
    out[:PIECE] = total.astype(BF)
    square = jnp.sum(total * total, 0, keepdims=True)
    terms = split_three(square)
    out[PIECE:] = jnp.concatenate(terms + (jnp.zeros((STAT - 3, 128), BF),), 0)


def sum_cross(own, r1, r2, r3):
    return pl.pallas_call(
        cross_kernel,
        out_shape=jax.ShapeDtypeStruct((PIECE + STAT, 128), BF),
        compiler_params=pltpu.CompilerParams(vmem_limit_bytes=8 << 20),
        cost_estimate=pl.CostEstimate(flops=600000, transcendentals=0, bytes_accessed=1200000),
        name="sum_cross",
    )(own, r1, r2, r3)


def split_three(x):
    high = x.astype(BF)
    rest = x - high.astype(F32)
    mid = rest.astype(BF)
    return high, mid, (rest - mid.astype(F32)).astype(BF)


def final_kernel(s_ref, *refs):
    pieces, later, out_hbm, dpk_hbm, dpv_hbm = refs[:8], refs[8], refs[9], refs[10], refs[11]
    bufs, outs, sem, out_sem = refs[12:]
    hand = [
        pltpu.make_async_copy(later.at[n], to, out_sem.at[8 + n]) for n, to in enumerate((dpk_hbm, dpv_hbm))
    ]
    for move in hand:
        move.start()
    segment, x, y, z = s_ref[0], s_ref[3], s_ref[4], s_ref[5]
    moves = [pltpu.make_async_copy(pieces[n], bufs.at[n], sem.at[n]) for n in range(8)]
    for move in moves:
        move.start()
    total = jnp.zeros((1, 128), F32)
    for n in range(8):
        moves[n].wait()
        for p in range(SIDE):
            stat = bufs[n, p, PIECE : PIECE + STAT, :].astype(F32)
            total = total + jnp.sum(stat, 0, keepdims=True)
    mean = jnp.sum(total, 1, keepdims=True) * (1.0 / (WIDTH * D))
    scale = jnp.minimum(1.0, 1.0 / jnp.sqrt(mean + 1e-06))
    writes = []
    for n in range(8):
        k = n % 4
        half = segment if n < 4 else 1 - segment
        quad = (jnp.where(half == 0, x, y) + SIDE - k) % SIDE
        at = jnp.where(half == 0, z, x)
        for p in range(SIDE):
            rows = pl.ds(pl.multiple_of((at + SIDE - p) % SIDE * SUB, 16), SUB)
            for tile in range(TILES):
                outs[n, rows, tile * 128 : tile * 128 + 128] = (
                    bufs[n, p, tile * SUB : tile * SUB + SUB, :].astype(F32) * scale
                ).astype(BF)
        write = pltpu.make_async_copy(
            outs.at[n],
            out_hbm.at[
                pl.ds(pl.multiple_of(quad * QUAD, 64), QUAD), pl.ds(pl.multiple_of(half * HALF, 128), HALF)
            ],
            out_sem.at[n],
        )
        write.start()
        writes.append(write)
    for write in writes + hand:
        write.wait()


def finish(scalars, pieces, later):
    any_spec = pl.BlockSpec(memory_space=pl.ANY)
    return pl.pallas_call(
        final_kernel,
        out_shape=(jax.ShapeDtypeStruct((WIDTH, D), BF),) + (jax.ShapeDtypeStruct((SUMS, WIDTH), BF),) * 2,
        grid_spec=pltpu.PrefetchScalarGridSpec(
            num_scalar_prefetch=1,
            grid=(1,),
            in_specs=[any_spec] * 9,
            out_specs=(any_spec,) * 3,
            scratch_shapes=[
                pltpu.VMEM((8, SIDE, PIECE + STAT, 128), BF),
                pltpu.VMEM((8, QUAD, HALF), BF),
                pltpu.SemaphoreType.DMA((8,)),
                pltpu.SemaphoreType.DMA((10,)),
            ],
        ),
        compiler_params=pltpu.CompilerParams(vmem_limit_bytes=32 << 20),
        cost_estimate=pl.CostEstimate(flops=7000000, transcendentals=0, bytes_accessed=14000000),
        name="clip",
    )(scalars, *pieces, later)


def hop(chip, axis, by):
    stride = {"x": 1, "y": SIDE, "z": SIDE * SIDE}[axis]
    at = (chip // stride) % SIDE
    return chip + (((at + by) % SIDE) - at) * stride


CHIPS = SIDE**3


def along(first, second, by):
    return [(c, hop(c, first, by)) for c in range(CHIPS)] + [
        (CHIPS + c, CHIPS + hop(c, second, by)) for c in range(CHIPS)
    ]


BOTH = ("seg", "dp")
SWAP = [(0, 1), (1, 0)]


def program(query_rows, key_rows, value_rows, prompt_keys, prompt_values, out_grad, w_out):
    q, k, v, grad_rows = query_rows[0], key_rows[0], value_rows[0], out_grad[0]
    grad_other = lax.ppermute(grad_rows, "seg", SWAP)
    where = jnp.stack([lax.axis_index("seg"), lax.axis_index("dp")]).astype(jnp.int32)
    scalars, prompt_keys, prompt_values = lax.optimization_barrier(
        (order_scalars(where), prompt_keys, prompt_values)
    )
    pk = lax.ppermute(prompt_keys[0], "seg", [(0, 1)])
    pv = lax.ppermute(prompt_values[0], "seg", [(0, 1)])

    attn, other, lses, sent = [], [], [], {}

    def forward(place, after=()):
        out, lse = forward_quad(place, scalars, q, k, v, pk, pv, after)
        attn.append(out)
        lses.append(lse)
        other.append(lax.ppermute(out, "seg", SWAP))

    def send(bys):
        parts = weight_quads(bys, scalars, attn, other, grad_rows, grad_other)
        for by, part in zip(bys, parts):
            sent[by] = lax.ppermute(part, BOTH, along("x", "y", by)) if by else part
        return parts

    forward(0)
    forward(1, (attn[0],))
    first = send((2,))
    forward(2, first)
    forward(3, first + [attn[2]])
    send((1, 3))
    send((0,))
    head_low = jnp.einsum("td,hd->th", grad_rows, w_out, preferred_element_type=F32).astype(BF)
    sent, head_low = lax.optimization_barrier((sent, head_low))
    own, *rest = sum_line(scalars, sent[0], sent[1], sent[2], sent[3])
    own = sum_mid(own, *[lax.ppermute(rest[by - 1], BOTH, along("z", "x", by)) for by in (1, 2, 3)])
    own = sum_cross(own, *[lax.ppermute(own, BOTH, along("y", "z", by)) for by in (1, 2, 3)])
    own = jnp.stack([own] + [lax.ppermute(own, BOTH, along("z", "x", by)) for by in (1, 2, 3)])

    own, head_low = lax.optimization_barrier((own, head_low))
    pieces = [own] + [lax.ppermute(own, BOTH, along("x", "y", by)) for by in (1, 2, 3)]
    dq, dk, dv, dp = backward(scalars, q, k, v, head_low, pk, pv, lses)
    pieces, dp = lax.optimization_barrier((pieces, dp))
    pieces = pieces + [lax.ppermute(part, "seg", SWAP) for part in pieces]
    weight_grad, dpk, dpv = finish(scalars, pieces, lax.ppermute(dp, "seg", [(1, 0)]))
    return (dq[None], dk[None], dv[None], dpk[None], dpv[None], weight_grad)


def solution(mesh):
    rows = P("dp", "seg", None)
    return jax.shard_map(
        program,
        mesh=mesh,
        in_specs=(rows,) * 6 + (P(),),
        out_specs=(rows,) * 5 + (P(),),
        check_vma=False,
    )
```

profile of v0, /device:TPU:1, one launch (start us, length us, event | category | flops | bytes accessed | tf_op | source)
XLA Modules:
  0.0 121.5 jit_solution(15217765103415727784)
XLA Ops:
  0.6 1.5 %collective-permute-start.4 = (bf16[512,2560]{1,0:T(8,128)(2,1)}, bf16[512,2560]{1,0:T(8,128)(2,1)S(1)}, u32[]{:S(2)}, u32[]{:S(2)}) collective-permute-start(bf16[512,2560]{1,0:T(8,128)(2,1)} %bitcast.24), channel_id=1, source_target_pairs={{0,64},{64,0},{1,65},{65,1},{2,66},{66,2},{3,67},{67,3},{4,68},{68... | collective-permute-start | bytes 7864328 | tf_op jit(solution)/shard_map/ppermute | solution.py:498
  2.1 0.1 pad_add_fusion.s_ref
  2.2 0.0 copy-start.3
  2.2 1.1 order.1.s_ref
  3.4 1.4 %collective-permute-start.1 = (bf16[50,1280]{1,0:T(8,128)(2,1)S(1)}, bf16[50,1280]{1,0:T(8,128)(2,1)S(1)}, u32[]{:S(2)}, u32[]{:S(2)}) collective-permute-start(bf16[50,1280]{1,0:T(8,128)(2,1)S(1)} %bitcast.55), channel_id=1, source_target_pairs={{0,64},{1,65},{2,66},{3,67},{4,68},{5,69},{6,70},{7,71},{8,72},{9,... | collective-permute-start | bytes 384008 | tf_op jit(solution)/shard_map/ppermute | solution.py:504
  4.8 1.3 %collective-permute-start = (bf16[50,1280]{1,0:T(8,128)(2,1)S(1)}, bf16[50,1280]{1,0:T(8,128)(2,1)S(1)}, u32[]{:S(2)}, u32[]{:S(2)}) collective-permute-start(bf16[50,1280]{1,0:T(8,128)(2,1)S(1)} %bitcast.56), channel_id=1, source_target_pairs={{0,64},{1,65},{2,66},{3,67},{4,68},{5,69},{6,70},{7,71},{8,72},{9,... | collective-permute-start | bytes 384008 | tf_op jit(solution)/shard_map/ppermute | solution.py:503
  6.1 0.8 collective-permute-done.1.pv_hbm.pv_in
  6.9 1.1 collective-permute-done.pk_hbm.pk_in
  8.1 2.9 %fwd_quad.4 = (bf16[320,512]{1,0:T(8,128)(2,1)S(1)}, f32[4,512]{1,0:T(4,128)S(1)}) custom-call(s32[10]{0:T(128)S(1)} %order.1.s_ref, bf16[512,1280]{1,0:T(8,128)(2,1)S(1)} %bitcast.28, bf16[512,1280]{1,0:T(8,128)(2,1)S(1)} %bitcast.33, bf16[512,1280]{1,0:T(8,128)(2,1)S(1)} %bitcast.38, bf16[50,1280]{1,0:T(8,128)(2,1)S(1)} %collective-permute-done.pk_hbm.pk_in, ...), custom_call_target="tpu_custom_call" | custom-call | flops 939524096 | bytes 1600000 | tf_op jit(solution)/shard_map/fwd_quad/pallas_call | solution.py:130
  11.0 0.0 copy-start
  11.0 2.9 %fwd_quad.5 = (bf16[320,512]{1,0:T(8,128)(2,1)S(1)}, f32[4,512]{1,0:T(4,128)S(1)}) custom-call(s32[10]{0:T(128)S(1)} %order.1.s_ref, bf16[512,1280]{1,0:T(8,128)(2,1)S(1)} %bitcast.29, bf16[512,1280]{1,0:T(8,128)(2,1)S(1)} %bitcast.34, bf16[512,1280]{1,0:T(8,128)(2,1)S(1)} %bitcast.39, bf16[50,1280]{1,0:T(8,128)(2,1)S(1)} %collective-permute-done.pk_hbm.pk_in, ...), custom_call_target="tpu_custom_call" | custom-call | flops 939524096 | bytes 1600000 | tf_op jit(solution)/shard_map/fwd_quad/pallas_call | solution.py:130
  13.9 0.2 collective-permute-start.3
  14.1 0.4 collective-permute-start.2
  14.5 1.1 collective-permute-done.3.refs_3_.refs_5_
  15.6 0.5 collective-permute-done.2.refs_2_.refs_4_
  16.1 0.0 collective-permute-done.4.refs_5_.refs_9_
  16.1 2.3 %weight_quads.3 = bf16[4,10,80,128]{3,2,1,0:T(8,128)(2,1)S(1)} custom-call(s32[10]{0:T(128)S(1)} %order.1.s_ref, bf16[320,512]{1,0:T(8,128)(2,1)S(1)} %get-tuple-element.45.rest_0_.refs_0_, bf16[320,512]{1,0:T(8,128)(2,1)S(1)} %get-tuple-element.46.refs_1_, bf16[320,512]{1,0:T(8,128)(2,1)S(1)} %collective-permute-done.2.refs_2_.refs_4_, ...), custom_call_target="tpu_custom_call" | custom-call | flops 838860800 | bytes 4200000 | tf_op jit(solution)/shard_map/weight_quads/pallas_call | solution.py:301
  18.4 2.9 %fwd_quad.6 = (bf16[320,512]{1,0:T(8,128)(2,1)S(1)}, f32[4,512]{1,0:T(4,128)S(1)}) custom-call(s32[10]{0:T(128)S(1)} %order.1.s_ref, bf16[512,1280]{1,0:T(8,128)(2,1)S(1)} %bitcast.30, bf16[512,1280]{1,0:T(8,128)(2,1)S(1)} %bitcast.35, bf16[512,1280]{1,0:T(8,128)(2,1)S(1)} %bitcast.40, bf16[50,1280]{1,0:T(8,128)(2,1)S(1)} %collective-permute-done.pk_hbm.pk_in, ...), custom_call_target="tpu_custom_call" | custom-call | flops 939524096 | bytes 1600000 | tf_op jit(solution)/shard_map/fwd_quad/pallas_call | solution.py:130
  21.3 0.0 slice-start
  21.3 2.9 %fwd_quad.7 = (bf16[320,512]{1,0:T(8,128)(2,1)S(1)}, f32[4,512]{1,0:T(4,128)S(1)}) custom-call(s32[10]{0:T(128)S(1)} %order.1.s_ref, bf16[512,1280]{1,0:T(8,128)(2,1)S(1)} %bitcast.31, bf16[512,1280]{1,0:T(8,128)(2,1)S(1)} %bitcast.36, bf16[512,1280]{1,0:T(8,128)(2,1)S(1)} %bitcast.41, bf16[50,1280]{1,0:T(8,128)(2,1)S(1)} %collective-permute-done.pk_hbm.pk_in, ...), custom_call_target="tpu_custom_call" | custom-call | flops 939524096 | bytes 1600000 | tf_op jit(solution)/shard_map/fwd_quad/pallas_call | solution.py:130
  24.2 0.0 slice-start.1
  24.2 0.2 collective-permute-start.6
  24.4 0.4 collective-permute-start.5
  24.8 3.0 %collective-permute-start.8 = (bf16[4,800,128]{2,1,0:T(8,128)(2,1)S(1)}, bf16[4,800,128]{2,1,0:T(8,128)(2,1)S(1)}, u32[]{:S(2)}, u32[]{:S(2)}) collective-permute-start(bf16[4,800,128]{2,1,0:T(8,128)(2,1)S(1)} %bitcast.45), channel_id=1, source_target_pairs={{0,2},{1,3},{2,0},{3,1},{4,6},{5,7},{6,4},{7,5},{8,10},{9,11},{10,... | collective-permute-start | bytes 2457608 | tf_op jit(solution)/shard_map/ppermute | solution.py:517
  27.8 0.0 collective-permute-done.6.refs_7_
  27.8 3.5 %weight_quads.5 = (bf16[4,10,80,128]{3,2,1,0:T(8,128)(2,1)S(1)}, bf16[4,10,80,128]{3,2,1,0:T(8,128)(2,1)S(1)}) custom-call(s32[10]{0:T(128)S(1)} %order.1.s_ref, bf16[320,512]{1,0:T(8,128)(2,1)S(1)} %get-tuple-element.45.rest_0_.refs_0_, bf16[320,512]{1,0:T(8,128)(2,1)S(1)} %get-tuple-element.46.refs_1_, ...), custom_call_target="tpu_custom_call" | custom-call | flops 1677721600 | bytes 4200000 | tf_op jit(solution)/shard_map/weight_quads/pallas_call | solution.py:301
  31.4 1.7 %collective-permute-start.9 = (bf16[4,800,128]{2,1,0:T(8,128)(2,1)S(1)}, bf16[4,800,128]{2,1,0:T(8,128)(2,1)S(1)}, u32[]{:S(2)}, u32[]{:S(2)}) collective-permute-start(bf16[4,800,128]{2,1,0:T(8,128)(2,1)S(1)} %bitcast.49), channel_id=1, source_target_pairs={{0,3},{1,0},{2,1},{3,2},{4,7},{5,4},{6,5},{7,6},{8,11},{9,8},{10,9... | collective-permute-start | bytes 2457608 | tf_op jit(solution)/shard_map/ppermute | solution.py:517
  33.0 0.1 collective-permute-start.7
  33.1 3.6 %convolution_convert_fusion.g_ref = bf16[512,1280]{1,0:T(8,128)(2,1)S(1)} fusion(bf16[1280,2560]{1,0:T(8,128)(2,1)S(1)} %bitcast.54, bf16[1,512,2560]{2,1,0:T(8,128)(2,1)S(1)} %copy-done), kind=kOutput, calls=%fused_computation | convolution fusion | flops 3356098560 | bytes 10485760 | tf_op jit(solution)/shard_map/td,hd->th/dot_general | solution.py:527
  36.7 2.4 %weight_quads.4 = f32[4,10,80,128]{3,2,1,0:T(8,128)S(1)} custom-call(s32[10]{0:T(128)S(1)} %order.1.s_ref, bf16[320,512]{1,0:T(8,128)(2,1)S(1)} %get-tuple-element.45.rest_0_.refs_0_, bf16[320,512]{1,0:T(8,128)(2,1)S(1)} %get-tuple-element.46.refs_1_, bf16[320,512]{1,0:T(8,128)(2,1)S(1)} %get-tuple-element.47.rest_1_.refs_2_, ...), custom_call_target="tpu_custom_call" | custom-call | flops 838860800 | bytes 4200000 | tf_op jit(solution)/shard_map/weight_quads/pallas_call | solution.py:301
  39.1 8.0 %collective-permute-done.9.r3 = bf16[4,800,128]{2,1,0:T(8,128)(2,1)S(1)} collective-permute-done((bf16[4,800,128]{2,1,0:T(8,128)(2,1)S(1)}, bf16[4,800,128]{2,1,0:T(8,128)(2,1)S(1)}, u32[]{:S(2)}, u32[]{:S(2)}) %collective-permute-start.9) | collective-permute-done | bytes 819232 | tf_op jit(solution)/shard_map/ppermute | solution.py:517
  47.1 1.3 %sum_line.1 = (f32[800,128]{1,0:T(8,128)S(1)}, bf16[800,128]{1,0:T(8,128)(2,1)S(1)}, bf16[800,128]{1,0:T(8,128)(2,1)S(1)}, bf16[800,128]{1,0:T(8,128)(2,1)S(1)}) custom-call(s32[10]{0:T(128)S(1)} %order.1.s_ref, f32[4,800,128]{2,1,0:T(8,128)S(1)} %bitcast.46, bf16[4,800,128]{2,1,0:T(8,128)(2,1)S(1)} %collective-permute-done.7.r1, ...), custom_call_target="tpu_custom_call" | custom-call | flops 2000000 | bytes 5000000 | tf_op jit(solution)/shard_map/sum_line/pallas_call | solution.py:357
  48.4 1.3 %collective-permute-start.10 = (bf16[800,128]{1,0:T(8,128)(2,1)S(1)}, bf16[800,128]{1,0:T(8,128)(2,1)S(1)}, u32[]{:S(2)}, u32[]{:S(2)}) collective-permute-start(bf16[800,128]{1,0:T(8,128)(2,1)S(1)} %get-tuple-element.56), channel_id=1, source_target_pairs={{0,16},{1,17},{2,18},{3,19},{4,20},{5,21},{6,22},{7,23},{8,24},{9,... | collective-permute-start | bytes 614408 | tf_op jit(solution)/shard_map/ppermute | solution.py:530
  49.7 2.4 %collective-permute-start.11 = (bf16[800,128]{1,0:T(8,128)(2,1)S(1)}, bf16[800,128]{1,0:T(8,128)(2,1)S(1)}, u32[]{:S(2)}, u32[]{:S(2)}) collective-permute-start(bf16[800,128]{1,0:T(8,128)(2,1)S(1)} %get-tuple-element.57), channel_id=1, source_target_pairs={{0,32},{1,33},{2,34},{3,35},{4,36},{5,37},{6,38},{7,39},{8,40},{9,... | collective-permute-start | bytes 614408 | tf_op jit(solution)/shard_map/ppermute | solution.py:530
  52.1 1.2 collective-permute-start.12
  53.3 1.3 %collective-permute-done.10.r1 = bf16[800,128]{1,0:T(8,128)(2,1)S(1)} collective-permute-done((bf16[800,128]{1,0:T(8,128)(2,1)S(1)}, bf16[800,128]{1,0:T(8,128)(2,1)S(1)}, u32[]{:S(2)}, u32[]{:S(2)}) %collective-permute-start.10) | collective-permute-done | bytes 204832 | tf_op jit(solution)/shard_map/ppermute | solution.py:530
  54.6 2.9 %collective-permute-done.11.r2 = bf16[800,128]{1,0:T(8,128)(2,1)S(1)} collective-permute-done((bf16[800,128]{1,0:T(8,128)(2,1)S(1)}, bf16[800,128]{1,0:T(8,128)(2,1)S(1)}, u32[]{:S(2)}, u32[]{:S(2)}) %collective-permute-start.11) | collective-permute-done | bytes 204832 | tf_op jit(solution)/shard_map/ppermute | solution.py:530
  57.5 0.1 sum_mid.1.own
  57.6 3.8 %collective-permute-start.15 = (bf16[800,128]{1,0:T(8,128)(2,1)S(1)}, bf16[800,128]{1,0:T(8,128)(2,1)S(1)}, u32[]{:S(2)}, u32[]{:S(2)}) collective-permute-start(bf16[800,128]{1,0:T(8,128)(2,1)S(1)} %sum_mid.1.own), channel_id=1, source_target_pairs={{0,12},{1,13},{2,14},{3,15},{4,0},{5,1},{6,2},{7,3},{8,4},{9,5},{1... | collective-permute-start | bytes 614408 | tf_op jit(solution)/shard_map/ppermute | solution.py:531
  61.4 0.7 collective-permute-start.13
  62.1 4.2 %collective-permute-done.15.r3 = bf16[800,128]{1,0:T(8,128)(2,1)S(1)} collective-permute-done((bf16[800,128]{1,0:T(8,128)(2,1)S(1)}, bf16[800,128]{1,0:T(8,128)(2,1)S(1)}, u32[]{:S(2)}, u32[]{:S(2)}) %collective-permute-start.15) | collective-permute-done | bytes 204832 | tf_op jit(solution)/shard_map/ppermute | solution.py:531
  66.3 1.3 %collective-permute-done.14.r2 = bf16[800,128]{1,0:T(8,128)(2,1)S(1)} collective-permute-done((bf16[800,128]{1,0:T(8,128)(2,1)S(1)}, bf16[800,128]{1,0:T(8,128)(2,1)S(1)}, u32[]{:S(2)}, u32[]{:S(2)}) %collective-permute-start.14) | collective-permute-done | bytes 204832 | tf_op jit(solution)/shard_map/ppermute | solution.py:531
  67.6 2.1 %collective-permute-done.13.r1 = bf16[800,128]{1,0:T(8,128)(2,1)S(1)} collective-permute-done((bf16[800,128]{1,0:T(8,128)(2,1)S(1)}, bf16[800,128]{1,0:T(8,128)(2,1)S(1)}, u32[]{:S(2)}, u32[]{:S(2)}) %collective-permute-start.13) | collective-permute-done | bytes 204832 | tf_op jit(solution)/shard_map/ppermute | solution.py:531
  69.7 0.1 sum_cross.1
  69.9 2.4 %collective-permute-start.18 = (bf16[808,128]{1,0:T(8,128)(2,1)S(1)}, bf16[808,128]{1,0:T(8,128)(2,1)S(1)}, u32[]{:S(2)}, u32[]{:S(2)}) collective-permute-start(bf16[808,128]{1,0:T(8,128)(2,1)S(1)} %sum_cross.1), channel_id=1, source_target_pairs={{0,48},{1,49},{2,50},{3,51},{4,52},{5,53},{6,54},{7,55},{8,56},{9,... | collective-permute-start | bytes 620552 | tf_op jit(solution)/shard_map/ppermute | solution.py:532
  72.2 0.9 collective-permute-start.17
  73.1 0.4 collective-permute-start.16
  73.5 3.7 %collective-permute-done.18 = bf16[808,128]{1,0:T(8,128)(2,1)S(1)} collective-permute-done((bf16[808,128]{1,0:T(8,128)(2,1)S(1)}, bf16[808,128]{1,0:T(8,128)(2,1)S(1)}, u32[]{:S(2)}, u32[]{:S(2)}) %collective-permute-start.18) | collective-permute-done | bytes 206880 | tf_op jit(solution)/shard_map/ppermute | solution.py:532
  77.2 1.3 %collective-permute-done.17 = bf16[808,128]{1,0:T(8,128)(2,1)S(1)} collective-permute-done((bf16[808,128]{1,0:T(8,128)(2,1)S(1)}, bf16[808,128]{1,0:T(8,128)(2,1)S(1)}, u32[]{:S(2)}, u32[]{:S(2)}) %collective-permute-start.17) | collective-permute-done | bytes 206880 | tf_op jit(solution)/shard_map/ppermute | solution.py:532
  78.5 2.4 %collective-permute-done.16 = bf16[808,128]{1,0:T(8,128)(2,1)S(1)} collective-permute-done((bf16[808,128]{1,0:T(8,128)(2,1)S(1)}, bf16[808,128]{1,0:T(8,128)(2,1)S(1)}, u32[]{:S(2)}, u32[]{:S(2)}) %collective-permute-start.16) | collective-permute-done | bytes 206880 | tf_op jit(solution)/shard_map/ppermute | solution.py:532
  80.9 0.1 pad_maximum_fusion.refs_0_
  81.0 2.4 %collective-permute-start.21 = (bf16[4,808,128]{2,1,0:T(8,128)(2,1)S(1)}, bf16[4,808,128]{2,1,0:T(8,128)(2,1)S(1)}, u32[]{:S(2)}, u32[]{:S(2)}) collective-permute-start(bf16[4,808,128]{2,1,0:T(8,128)(2,1)S(1)} %pad_maximum_fusion.refs_0_), channel_id=1, source_target_pairs={{0,3},{1,0},{2,1},{3,2},{4,7},{5,4},{6,5},{7,6},{8,11},{9,8},{10,9... | collective-permute-start | bytes 2482184 | tf_op jit(solution)/shard_map/ppermute | solution.py:535
  83.4 0.3 collective-permute-start.20
  83.7 0.4 collective-permute-start.19
  84.1 16.6 %attend_back.1 = (bf16[512,1280]{1,0:T(8,128)(2,1)}, bf16[512,1280]{1,0:T(8,128)(2,1)}, bf16[512,1280]{1,0:T(8,128)(2,1)}, bf16[2,50,1280]{2,1,0:T(8,128)(2,1)S(1)}) custom-call(s32[10]{0:T(128)S(1)} %order.1.s_ref, bf16[512,1280]{1,0:T(8,128)(2,1)S(1)} %bitcast.32, bf16[512,1280]{1,0:T(8,128)(2,1)S(1)} %bitcast.37, bf16[512,1280]{1,0:T(8,128)(2,1)S(1)} %bitcast.42, ...), custom_call_target="tpu_custom_call" | custom-call | flops 9395240960 | bytes 10000000 | tf_op jit(solution)/shard_map/attend_back/pallas_call | solution.py:243
  100.7 0.9 collective-permute-done.21.refs_3_
  101.6 3.7 %collective-permute-done.19.refs_1_ = bf16[4,808,128]{2,1,0:T(8,128)(2,1)S(1)} collective-permute-done((bf16[4,808,128]{2,1,0:T(8,128)(2,1)S(1)}, bf16[4,808,128]{2,1,0:T(8,128)(2,1)S(1)}, u32[]{:S(2)}, u32[]{:S(2)}) %collective-permute-start.19) | collective-permute-done | bytes 827424 | tf_op jit(solution)/shard_map/ppermute | solution.py:535
  105.3 5.4 %collective-permute-start.22 = (bf16[4,808,128]{2,1,0:T(8,128)(2,1)S(1)}, bf16[4,808,128]{2,1,0:T(8,128)(2,1)S(1)}, u32[]{:S(2)}, u32[]{:S(2)}) collective-permute-start(bf16[4,808,128]{2,1,0:T(8,128)(2,1)S(1)} %pad_maximum_fusion.refs_0_), channel_id=1, source_target_pairs={{0,64},{64,0},{1,65},{65,1},{2,66},{66,2},{3,67},{67,3},{4,68},{68... | collective-permute-start | bytes 2482184 | tf_op jit(solution)/shard_map/ppermute | solution.py:538
  110.8 0.0 collective-permute-start.23
  110.8 0.5 collective-permute-start.24
  111.3 0.0 collective-permute-start.25
  111.3 2.4 %collective-permute-start.26 = (bf16[2,50,1280]{2,1,0:T(8,128)(2,1)S(1)}, bf16[2,50,1280]{2,1,0:T(8,128)(2,1)S(1)}, u32[]{:S(2)}, u32[]{:S(2)}) collective-permute-start(bf16[2,50,1280]{2,1,0:T(8,128)(2,1)S(1)} %get-tuple-element.74), channel_id=1, source_target_pairs={{64,0},{65,1},{66,2},{67,3},{68,4},{69,5},{70,6},{71,7},{72,8},{73... | collective-permute-start | bytes 768008 | tf_op jit(solution)/shard_map/ppermute | solution.py:539
  113.7 3.0 %collective-permute-done.26.refs_8_ = bf16[2,50,1280]{2,1,0:T(8,128)(2,1)S(1)} collective-permute-done((bf16[2,50,1280]{2,1,0:T(8,128)(2,1)S(1)}, bf16[2,50,1280]{2,1,0:T(8,128)(2,1)S(1)}, u32[]{:S(2)}, u32[]{:S(2)}) %collective-permute-start.26) | collective-permute-done | bytes 256032 | tf_op jit(solution)/shard_map/ppermute | solution.py:539
  116.7 4.6 %clip.1 = (bf16[1280,2560]{1,0:T(8,128)(2,1)}, bf16[50,1280]{1,0:T(8,128)(2,1)}, bf16[50,1280]{1,0:T(8,128)(2,1)}) custom-call(s32[10]{0:T(128)S(1)} %order.1.s_ref, bf16[4,808,128]{2,1,0:T(8,128)(2,1)S(1)} %pad_maximum_fusion.refs_0_, bf16[4,808,128]{2,1,0:T(8,128)(2,1)S(1)} %collective-permute-done.19.refs_1_, ...), custom_call_target="tpu_custom_call" | custom-call | flops 7000000 | bytes 14000000 | tf_op jit(solution)/shard_map/clip/pallas_call | solution.py:456
  (23 shorter events, 0.1 us)
Async XLA Ops:
  0.6 15.4 %collective-permute-start.4 = (bf16[512,2560]{1,0:T(8,128)(2,1)}, bf16[512,2560]{1,0:T(8,128)(2,1)S(1)}, u32[]{:S(2)}, u32[]{:S(2)}) collective-permute-start(bf16[512,2560]{1,0:T(8,128)(2,1)} %bitcast.24), channel_id=1, source_target_pairs={{0,64},{64,0},{1,65},{65,1},{2,66},{66,2},{3,67},{67,3},{4,68},{68... | collective-permute-start | bytes 7864328 | tf_op jit(solution)/shard_map/ppermute | solution.py:498
  2.2 1.2 copy-start.4
  2.2 2.6 %copy-start.5 = (bf16[1,50,1280]{2,1,0:T(8,128)(2,1)S(1)}, bf16[1,50,1280]{2,1,0:T(8,128)(2,1)}, u32[]{:S(2)}) copy-start(bf16[1,50,1280]{2,1,0:T(8,128)(2,1)} %param.10) | copy-start | bytes 384004
  2.2 5.9 %copy-start.1 = (bf16[1,512,1280]{2,1,0:T(8,128)(2,1)S(1)}, bf16[1,512,1280]{2,1,0:T(8,128)(2,1)}, u32[]{:S(2)}) copy-start(bf16[1,512,1280]{2,1,0:T(8,128)(2,1)} %param.7) | copy-start | bytes 3932164
  2.2 5.9 %copy-start.2 = (bf16[1,512,1280]{2,1,0:T(8,128)(2,1)S(1)}, bf16[1,512,1280]{2,1,0:T(8,128)(2,1)}, u32[]{:S(2)}) copy-start(bf16[1,512,1280]{2,1,0:T(8,128)(2,1)} %param.8) | copy-start | bytes 3932164
  2.2 5.9 %copy-start.3 = (bf16[1,512,1280]{2,1,0:T(8,128)(2,1)S(1)}, bf16[1,512,1280]{2,1,0:T(8,128)(2,1)}, u32[]{:S(2)}) copy-start(bf16[1,512,1280]{2,1,0:T(8,128)(2,1)} %param.9) | copy-start | bytes 3932164
  3.4 3.6 %collective-permute-start.1 = (bf16[50,1280]{1,0:T(8,128)(2,1)S(1)}, bf16[50,1280]{1,0:T(8,128)(2,1)S(1)}, u32[]{:S(2)}, u32[]{:S(2)}) collective-permute-start(bf16[50,1280]{1,0:T(8,128)(2,1)S(1)} %bitcast.55), channel_id=1, source_target_pairs={{0,64},{1,65},{2,66},{3,67},{4,68},{5,69},{6,70},{7,71},{8,72},{9,... | collective-permute-start | bytes 384008 | tf_op jit(solution)/shard_map/ppermute | solution.py:504
  4.8 3.3 %collective-permute-start = (bf16[50,1280]{1,0:T(8,128)(2,1)S(1)}, bf16[50,1280]{1,0:T(8,128)(2,1)S(1)}, u32[]{:S(2)}, u32[]{:S(2)}) collective-permute-start(bf16[50,1280]{1,0:T(8,128)(2,1)S(1)} %bitcast.56), channel_id=1, source_target_pairs={{0,64},{1,65},{2,66},{3,67},{4,68},{5,69},{6,70},{7,71},{8,72},{9,... | collective-permute-start | bytes 384008 | tf_op jit(solution)/shard_map/ppermute | solution.py:503
  11.0 5.1 %copy-start = (bf16[1,512,2560]{2,1,0:T(8,128)(2,1)S(1)}, bf16[1,512,2560]{2,1,0:T(8,128)(2,1)}, u32[]{:S(2)}) copy-start(bf16[1,512,2560]{2,1,0:T(8,128)(2,1)} %param.12) | copy-start | bytes 7864324
  13.9 1.7 %collective-permute-start.3 = (bf16[320,512]{1,0:T(8,128)(2,1)S(1)}, bf16[320,512]{1,0:T(8,128)(2,1)S(1)}, u32[]{:S(2)}, u32[]{:S(2)}) collective-permute-start(bf16[320,512]{1,0:T(8,128)(2,1)S(1)} %get-tuple-element.46.refs_1_), channel_id=1, source_target_pairs={{0,64},{64,0},{1,65},{65,1},{2,66},{66,2},{3,67},{67,3},{4,68},{68... | collective-permute-start | bytes 983048 | tf_op jit(solution)/shard_map/ppermute | solution.py:512
  14.1 2.0 %collective-permute-start.2 = (bf16[320,512]{1,0:T(8,128)(2,1)S(1)}, bf16[320,512]{1,0:T(8,128)(2,1)S(1)}, u32[]{:S(2)}, u32[]{:S(2)}) collective-permute-start(bf16[320,512]{1,0:T(8,128)(2,1)S(1)} %get-tuple-element.45.rest_0_.refs_0_), channel_id=1, source_target_pairs={{0,64},{64,0},{1,65},{65,1},{2,66},{66,2},{3,67},{67,3},{4,68},{68... | collective-permute-start | bytes 983048 | tf_op jit(solution)/shard_map/ppermute | solution.py:512
  21.3 11.8 %slice-start = ((s8[6553600]{0:T(1024)(128)(4,1)}), s8[4194304]{0:T(1024)(128)(4,1)S(1)}, s32[]{:S(2)}) async-start(s8[6553600]{0:T(1024)(128)(4,1)} %bitcast.53), calls=%async_computation | async-start | bytes 8388608
  24.2 8.9 %slice-start.1 = ((s8[6553600]{0:T(1024)(128)(4,1)}), s8[2359296]{0:T(1024)(128)(4,1)S(1)}, s32[]{:S(2)}) async-start(s8[6553600]{0:T(1024)(128)(4,1)} %bitcast.53), calls=%async_computation.1 | async-start | bytes 4718592
  24.2 3.6 %collective-permute-start.6 = (bf16[320,512]{1,0:T(8,128)(2,1)S(1)}, bf16[320,512]{1,0:T(8,128)(2,1)S(1)}, u32[]{:S(2)}, u32[]{:S(2)}) collective-permute-start(bf16[320,512]{1,0:T(8,128)(2,1)S(1)} %get-tuple-element.48.refs_3_), channel_id=1, source_target_pairs={{0,64},{64,0},{1,65},{65,1},{2,66},{66,2},{3,67},{67,3},{4,68},{68... | collective-permute-start | bytes 983048 | tf_op jit(solution)/shard_map/ppermute | solution.py:512
  24.4 3.4 %collective-permute-start.5 = (bf16[320,512]{1,0:T(8,128)(2,1)S(1)}, bf16[320,512]{1,0:T(8,128)(2,1)S(1)}, u32[]{:S(2)}, u32[]{:S(2)}) collective-permute-start(bf16[320,512]{1,0:T(8,128)(2,1)S(1)} %get-tuple-element.47.rest_1_.refs_2_), channel_id=1, source_target_pairs={{0,64},{64,0},{1,65},{65,1},{2,66},{66,2},{3,67},{67,3},{4,68},{68... | collective-permute-start | bytes 983048 | tf_op jit(solution)/shard_map/ppermute | solution.py:512
  24.8 14.3 %collective-permute-start.8 = (bf16[4,800,128]{2,1,0:T(8,128)(2,1)S(1)}, bf16[4,800,128]{2,1,0:T(8,128)(2,1)S(1)}, u32[]{:S(2)}, u32[]{:S(2)}) collective-permute-start(bf16[4,800,128]{2,1,0:T(8,128)(2,1)S(1)} %bitcast.45), channel_id=1, source_target_pairs={{0,2},{1,3},{2,0},{3,1},{4,6},{5,7},{6,4},{7,5},{8,10},{9,11},{10,... | collective-permute-start | bytes 2457608 | tf_op jit(solution)/shard_map/ppermute | solution.py:517
  31.4 15.7 %collective-permute-start.9 = (bf16[4,800,128]{2,1,0:T(8,128)(2,1)S(1)}, bf16[4,800,128]{2,1,0:T(8,128)(2,1)S(1)}, u32[]{:S(2)}, u32[]{:S(2)}) collective-permute-start(bf16[4,800,128]{2,1,0:T(8,128)(2,1)S(1)} %bitcast.49), channel_id=1, source_target_pairs={{0,3},{1,0},{2,1},{3,2},{4,7},{5,4},{6,5},{7,6},{8,11},{9,8},{10,9... | collective-permute-start | bytes 2457608 | tf_op jit(solution)/shard_map/ppermute | solution.py:517
  33.0 14.0 %collective-permute-start.7 = (bf16[4,800,128]{2,1,0:T(8,128)(2,1)S(1)}, bf16[4,800,128]{2,1,0:T(8,128)(2,1)S(1)}, u32[]{:S(2)}, u32[]{:S(2)}) collective-permute-start(bf16[4,800,128]{2,1,0:T(8,128)(2,1)S(1)} %bitcast.48), channel_id=1, source_target_pairs={{0,1},{1,2},{2,3},{3,0},{4,5},{5,6},{6,7},{7,4},{8,9},{9,10},{10,1... | collective-permute-start | bytes 2457608 | tf_op jit(solution)/shard_map/ppermute | solution.py:517
  48.4 6.2 %collective-permute-start.10 = (bf16[800,128]{1,0:T(8,128)(2,1)S(1)}, bf16[800,128]{1,0:T(8,128)(2,1)S(1)}, u32[]{:S(2)}, u32[]{:S(2)}) collective-permute-start(bf16[800,128]{1,0:T(8,128)(2,1)S(1)} %get-tuple-element.56), channel_id=1, source_target_pairs={{0,16},{1,17},{2,18},{3,19},{4,20},{5,21},{6,22},{7,23},{8,24},{9,... | collective-permute-start | bytes 614408 | tf_op jit(solution)/shard_map/ppermute | solution.py:530
  49.7 7.8 %collective-permute-start.11 = (bf16[800,128]{1,0:T(8,128)(2,1)S(1)}, bf16[800,128]{1,0:T(8,128)(2,1)S(1)}, u32[]{:S(2)}, u32[]{:S(2)}) collective-permute-start(bf16[800,128]{1,0:T(8,128)(2,1)S(1)} %get-tuple-element.57), channel_id=1, source_target_pairs={{0,32},{1,33},{2,34},{3,35},{4,36},{5,37},{6,38},{7,39},{8,40},{9,... | collective-permute-start | bytes 614408 | tf_op jit(solution)/shard_map/ppermute | solution.py:530
  52.1 5.3 %collective-permute-start.12 = (bf16[800,128]{1,0:T(8,128)(2,1)S(1)}, bf16[800,128]{1,0:T(8,128)(2,1)S(1)}, u32[]{:S(2)}, u32[]{:S(2)}) collective-permute-start(bf16[800,128]{1,0:T(8,128)(2,1)S(1)} %get-tuple-element.58), channel_id=1, source_target_pairs={{0,48},{1,49},{2,50},{3,51},{4,52},{5,53},{6,54},{7,55},{8,56},{9,... | collective-permute-start | bytes 614408 | tf_op jit(solution)/shard_map/ppermute | solution.py:530
  57.6 8.7 %collective-permute-start.15 = (bf16[800,128]{1,0:T(8,128)(2,1)S(1)}, bf16[800,128]{1,0:T(8,128)(2,1)S(1)}, u32[]{:S(2)}, u32[]{:S(2)}) collective-permute-start(bf16[800,128]{1,0:T(8,128)(2,1)S(1)} %sum_mid.1.own), channel_id=1, source_target_pairs={{0,12},{1,13},{2,14},{3,15},{4,0},{5,1},{6,2},{7,3},{8,4},{9,5},{1... | collective-permute-start | bytes 614408 | tf_op jit(solution)/shard_map/ppermute | solution.py:531
  61.4 6.2 %collective-permute-start.14 = (bf16[800,128]{1,0:T(8,128)(2,1)S(1)}, bf16[800,128]{1,0:T(8,128)(2,1)S(1)}, u32[]{:S(2)}, u32[]{:S(2)}) collective-permute-start(bf16[800,128]{1,0:T(8,128)(2,1)S(1)} %sum_mid.1.own), channel_id=1, source_target_pairs={{0,8},{1,9},{2,10},{3,11},{4,12},{5,13},{6,14},{7,15},{8,0},{9,1},... | collective-permute-start | bytes 614408 | tf_op jit(solution)/shard_map/ppermute | solution.py:531
  61.4 8.3 %collective-permute-start.13 = (bf16[800,128]{1,0:T(8,128)(2,1)S(1)}, bf16[800,128]{1,0:T(8,128)(2,1)S(1)}, u32[]{:S(2)}, u32[]{:S(2)}) collective-permute-start(bf16[800,128]{1,0:T(8,128)(2,1)S(1)} %sum_mid.1.own), channel_id=1, source_target_pairs={{0,4},{1,5},{2,6},{3,7},{4,8},{5,9},{6,10},{7,11},{8,12},{9,13},{1... | collective-permute-start | bytes 614408 | tf_op jit(solution)/shard_map/ppermute | solution.py:531
  69.9 7.3 %collective-permute-start.18 = (bf16[808,128]{1,0:T(8,128)(2,1)S(1)}, bf16[808,128]{1,0:T(8,128)(2,1)S(1)}, u32[]{:S(2)}, u32[]{:S(2)}) collective-permute-start(bf16[808,128]{1,0:T(8,128)(2,1)S(1)} %sum_cross.1), channel_id=1, source_target_pairs={{0,48},{1,49},{2,50},{3,51},{4,52},{5,53},{6,54},{7,55},{8,56},{9,... | collective-permute-start | bytes 620552 | tf_op jit(solution)/shard_map/ppermute | solution.py:532
  72.2 6.2 %collective-permute-start.17 = (bf16[808,128]{1,0:T(8,128)(2,1)S(1)}, bf16[808,128]{1,0:T(8,128)(2,1)S(1)}, u32[]{:S(2)}, u32[]{:S(2)}) collective-permute-start(bf16[808,128]{1,0:T(8,128)(2,1)S(1)} %sum_cross.1), channel_id=1, source_target_pairs={{0,32},{1,33},{2,34},{3,35},{4,36},{5,37},{6,38},{7,39},{8,40},{9,... | collective-permute-start | bytes 620552 | tf_op jit(solution)/shard_map/ppermute | solution.py:532
  73.1 7.8 %collective-permute-start.16 = (bf16[808,128]{1,0:T(8,128)(2,1)S(1)}, bf16[808,128]{1,0:T(8,128)(2,1)S(1)}, u32[]{:S(2)}, u32[]{:S(2)}) collective-permute-start(bf16[808,128]{1,0:T(8,128)(2,1)S(1)} %sum_cross.1), channel_id=1, source_target_pairs={{0,16},{1,17},{2,18},{3,19},{4,20},{5,21},{6,22},{7,23},{8,24},{9,... | collective-permute-start | bytes 620552 | tf_op jit(solution)/shard_map/ppermute | solution.py:532
  81.0 20.7 %collective-permute-start.21 = (bf16[4,808,128]{2,1,0:T(8,128)(2,1)S(1)}, bf16[4,808,128]{2,1,0:T(8,128)(2,1)S(1)}, u32[]{:S(2)}, u32[]{:S(2)}) collective-permute-start(bf16[4,808,128]{2,1,0:T(8,128)(2,1)S(1)} %pad_maximum_fusion.refs_0_), channel_id=1, source_target_pairs={{0,3},{1,0},{2,1},{3,2},{4,7},{5,4},{6,5},{7,6},{8,11},{9,8},{10,9... | collective-permute-start | bytes 2482184 | tf_op jit(solution)/shard_map/ppermute | solution.py:535
  83.4 18.2 %collective-permute-start.20 = (bf16[4,808,128]{2,1,0:T(8,128)(2,1)S(1)}, bf16[4,808,128]{2,1,0:T(8,128)(2,1)S(1)}, u32[]{:S(2)}, u32[]{:S(2)}) collective-permute-start(bf16[4,808,128]{2,1,0:T(8,128)(2,1)S(1)} %pad_maximum_fusion.refs_0_), channel_id=1, source_target_pairs={{0,2},{1,3},{2,0},{3,1},{4,6},{5,7},{6,4},{7,5},{8,10},{9,11},{10,... | collective-permute-start | bytes 2482184 | tf_op jit(solution)/shard_map/ppermute | solution.py:535
  83.7 21.6 %collective-permute-start.19 = (bf16[4,808,128]{2,1,0:T(8,128)(2,1)S(1)}, bf16[4,808,128]{2,1,0:T(8,128)(2,1)S(1)}, u32[]{:S(2)}, u32[]{:S(2)}) collective-permute-start(bf16[4,808,128]{2,1,0:T(8,128)(2,1)S(1)} %pad_maximum_fusion.refs_0_), channel_id=1, source_target_pairs={{0,1},{1,2},{2,3},{3,0},{4,5},{5,6},{6,7},{7,4},{8,9},{9,10},{10,1... | collective-permute-start | bytes 2482184 | tf_op jit(solution)/shard_map/ppermute | solution.py:535
  105.3 11.4 %collective-permute-start.22 = (bf16[4,808,128]{2,1,0:T(8,128)(2,1)S(1)}, bf16[4,808,128]{2,1,0:T(8,128)(2,1)S(1)}, u32[]{:S(2)}, u32[]{:S(2)}) collective-permute-start(bf16[4,808,128]{2,1,0:T(8,128)(2,1)S(1)} %pad_maximum_fusion.refs_0_), channel_id=1, source_target_pairs={{0,64},{64,0},{1,65},{65,1},{2,66},{66,2},{3,67},{67,3},{4,68},{68... | collective-permute-start | bytes 2482184 | tf_op jit(solution)/shard_map/ppermute | solution.py:538
  110.8 5.9 %collective-permute-start.23 = (bf16[4,808,128]{2,1,0:T(8,128)(2,1)S(1)}, bf16[4,808,128]{2,1,0:T(8,128)(2,1)S(1)}, u32[]{:S(2)}, u32[]{:S(2)}) collective-permute-start(bf16[4,808,128]{2,1,0:T(8,128)(2,1)S(1)} %collective-permute-done.19.refs_1_), channel_id=1, source_target_pairs={{0,64},{64,0},{1,65},{65,1},{2,66},{66,2},{3,67},{67,3},{4,68},{68... | collective-permute-start | bytes 2482184 | tf_op jit(solution)/shard_map/ppermute | solution.py:538
  110.8 5.9 %collective-permute-start.24 = (bf16[4,808,128]{2,1,0:T(8,128)(2,1)S(1)}, bf16[4,808,128]{2,1,0:T(8,128)(2,1)S(1)}, u32[]{:S(2)}, u32[]{:S(2)}) collective-permute-start(bf16[4,808,128]{2,1,0:T(8,128)(2,1)S(1)} %collective-permute-done.20.refs_2_), channel_id=1, source_target_pairs={{0,64},{64,0},{1,65},{65,1},{2,66},{66,2},{3,67},{67,3},{4,68},{68... | collective-permute-start | bytes 2482184 | tf_op jit(solution)/shard_map/ppermute | solution.py:538
  111.3 5.4 %collective-permute-start.25 = (bf16[4,808,128]{2,1,0:T(8,128)(2,1)S(1)}, bf16[4,808,128]{2,1,0:T(8,128)(2,1)S(1)}, u32[]{:S(2)}, u32[]{:S(2)}) collective-permute-start(bf16[4,808,128]{2,1,0:T(8,128)(2,1)S(1)} %collective-permute-done.21.refs_3_), channel_id=1, source_target_pairs={{0,64},{64,0},{1,65},{65,1},{2,66},{66,2},{3,67},{67,3},{4,68},{68... | collective-permute-start | bytes 2482184 | tf_op jit(solution)/shard_map/ppermute | solution.py:538
  111.3 5.4 %collective-permute-start.26 = (bf16[2,50,1280]{2,1,0:T(8,128)(2,1)S(1)}, bf16[2,50,1280]{2,1,0:T(8,128)(2,1)S(1)}, u32[]{:S(2)}, u32[]{:S(2)}) collective-permute-start(bf16[2,50,1280]{2,1,0:T(8,128)(2,1)S(1)} %get-tuple-element.74), channel_id=1, source_target_pairs={{64,0},{65,1},{66,2},{67,3},{68,4},{69,5},{70,6},{71,7},{72,8},{73... | collective-permute-start | bytes 768008 | tf_op jit(solution)/shard_map/ppermute | solution.py:539
where the time goes:
time: 122 us
  Pallas kernels  43.8 us (36%)
  waiting for transfers between devices  38.3 us (31%)
  starting transfers between devices  34.7 us (28%)
  matrix products  3.59 us (3%)
    pallas_call x1, Pallas kernels, backward(): pl.pallas_call(bwd_kernel, out_shape=(jax.ShapeDtypeStruct((TOK, WIDTH),...  16.6 us
    pallas_call x4, Pallas kernels, forward_quad(): pl.pallas_call(functools.partial(fwd_kernel, place), out_shape=(jax.Shape...  11.6 us
    pallas_call x3, Pallas kernels, weight_quads(): pl.pallas_call(functools.partial(weight_kernel, bys, places), out_shape=[...  8.24 us
    ppermute x3, waiting for transfers between devices, send(): sent[by] = lax.ppermute(part, BOTH, along('x', 'y', by)) if by else part  7.96 us
    ppermute x3, waiting for transfers between devices, program(): lax.ppermute(own, BOTH, along('y', 'z', by))  7.59 us
    ppermute x3, waiting for transfers between devices, program(): lax.ppermute(own, BOTH, along('z', 'x', by))  7.4 us
    ppermute x4, starting transfers between devices, program(): pieces = pieces + [lax.ppermute(part, 'seg', SWAP) for part in pieces]  5.94 us
    ppermute x3, starting transfers between devices, program(): lax.ppermute(rest[by - 1], BOTH, along('z', 'x', by))  4.89 us
  transfers between devices with their start and end apart: 27, of which 16 were waited for; matrix products, arithmetic and copies ran while one was open for 3% of the time, Pallas kernels for 24%

commit v1 on v0

--- a/solution.py
+++ b/solution.py
@@ -45,48 +45,28 @@
     return lax.broadcasted_iota(jnp.int32, shape, dim)
 
 
-def fwd_kernel(place, s_ref, q_hbm, k_hbm, v_hbm, pk_hbm, pv_hbm, *rest):
-    o_ref, lse_ref, q_ref, k_ref, v_ref, pk_ref, pv_ref, vt_ref, pvt_ref, pk_in, pv_in, sem = rest[-12:]
-    segment = s_ref[0]
-    quad = s_ref[ORDER + place]
+def fwd_kernel(place, s_ref, q_ref, k_ref, v_ref, prompt_ref, *rest):
+    o_ref, lse_ref, pk_ref, vt_ref, pvt_ref = rest[-5:]
+    segment, quad = s_ref[0], s_ref[ORDER + place]
     odd = quad & 1
-    window = pl.ds(pl.multiple_of(((quad * 5) >> 1) * 128, 128), WIN)
-    pk_ref[...] = jnp.zeros_like(pk_ref)
-    pv_ref[...] = jnp.zeros_like(pv_ref)
-    moves = [
-        pltpu.make_async_copy(src.at[:, window], dst, sem.at[n])
-        for n, (src, dst) in enumerate(
-            (
-                (q_hbm, q_ref),
-                (k_hbm, k_ref),
-                (pk_hbm, pk_in),
-                (v_hbm, v_ref),
-                (pv_hbm, pv_in),
-            )
-        )
-    ]
-    for move in moves:
-        move.start()
-    for move in moves[:3]:
-        move.wait()
-    pk_ref[:SUMS] = pk_in[...]
-    for move in moves[3:]:
-        move.wait()
-    pv_ref[:SUMS] = pv_in[...]
-    vt_ref[...] = jnp.transpose(v_ref[...])
-    pvt_ref[...] = jnp.transpose(pv_ref[...])
+    start = ((quad * 5) >> 1) * 128
+    window = pl.ds(pl.multiple_of(start, 128), WIN)
+    rows = jnp.zeros((PAD - SUMS, WIN), BF)
+    pk_ref[...] = jnp.concatenate([prompt_ref[0, :, window], rows], 0)
+    vt_ref[...] = jnp.transpose(v_ref[:, window])
+    pvt_ref[...] = jnp.transpose(jnp.concatenate([prompt_ref[1, :, window], rows], 0))
     lanes = iota((TOK, BLK), 1)
     causal = iota((BLK, BLK), 0) <= iota((BLK, BLK), 1)
     seen = iota((PAD, TOK), 0) < SUMS * segment
 
     def head(h, at):
         low = 64 * odd + HD * h - at
-        w = pl.ds(at, BLK)
+        w = pl.ds(pl.multiple_of(start + at, 128), BLK)
         mine = (lanes >= low) & (lanes < low + HD)
         qm = jnp.where(mine, q_ref[:, w], jnp.zeros((), BF))
         s0 = dot_nt(k_ref[:BLK, w], qm)
         s1 = dot_nt(k_ref[BLK:, w], qm[BLK:])
-        sp = jnp.where(seen, dot_nt(pk_ref[:, w], qm), NEG)
+        sp = jnp.where(seen, dot_nt(pk_ref[:, at : at + BLK], qm), NEG)
         s00 = jnp.where(causal, s0[:, :BLK], NEG)
         s01 = s0[:, BLK:]
         s11 = jnp.where(causal, s1, NEG)
@@ -125,45 +105,30 @@
         head(h, h // 2 * 128)
 
 
-def forward_quad(place, scalars, q, k, v, pk, pv, after):
-    any_spec = pl.BlockSpec(memory_space=pl.ANY)
+def forward_quad(place, scalars, q, k, v, prompts, after):
+    vmem = pl.BlockSpec(memory_space=pltpu.VMEM)
     return pl.pallas_call(
         functools.partial(fwd_kernel, place),
-        out_shape=(
-            jax.ShapeDtypeStruct((QUAD, TOK), BF),
-            jax.ShapeDtypeStruct((4, TOK), F32),
-        ),
-        grid_spec=pltpu.PrefetchScalarGridSpec(
-            num_scalar_prefetch=1,
-            grid=(1,),
-            in_specs=[any_spec] * (5 + len(after)),
-            out_specs=(
-                pl.BlockSpec((QUAD, TOK), lambda i, s: (0, 0)),
-                pl.BlockSpec((4, TOK), lambda i, s: (0, 0)),
-            ),
-            scratch_shapes=[
-                pltpu.VMEM((TOK, WIN), BF),
-                pltpu.VMEM((TOK, WIN), BF),
-                pltpu.VMEM((TOK, WIN), BF),
-                pltpu.VMEM((PAD, WIN), BF),
-                pltpu.VMEM((PAD, WIN), BF),
-                pltpu.VMEM((WIN, TOK), BF),
-                pltpu.VMEM((WIN, PAD), BF),
-                pltpu.VMEM((SUMS, WIN), BF),
-                pltpu.VMEM((SUMS, WIN), BF),
-                pltpu.SemaphoreType.DMA((5,)),
-            ],
-        ),
+        out_shape=(jax.ShapeDtypeStruct((QUAD, TOK), BF), jax.ShapeDtypeStruct((4, TOK), F32)),
+        in_specs=[pl.BlockSpec(memory_space=pltpu.SMEM)]
+        + [vmem] * 4
+        + [pl.BlockSpec(memory_space=pl.ANY)] * len(after),
+        out_specs=(vmem, vmem),
+        scratch_shapes=[
+            pltpu.VMEM((PAD, WIN), BF),
+            pltpu.VMEM((WIN, TOK), BF),
+            pltpu.VMEM((WIN, PAD), BF),
+        ],
         compiler_params=pltpu.CompilerParams(vmem_limit_bytes=24 << 20),
         cost_estimate=pl.CostEstimate(
             flops=4 * 2 * 2 * 896 * 256 * 256, transcendentals=4 * 896 * 256, bytes_accessed=1600000
         ),
         name="fwd_quad",
-    )(scalars, q, k, v, pk, pv, *after)
+    )(scalars, q, k, v, prompts, *after)
 
 
 def bwd_kernel(
-    s_ref, q_ref, k_ref, v_ref, g_ref, pk_in, pv_in, lse_0, lse_1, lse_2, lse_3,
+    s_ref, q_ref, k_ref, v_ref, g_ref, prompt_ref, lse_0, lse_1, lse_2, lse_3,
     dq_ref, dk_ref, dv_ref, dp_ref,
     kt_ref, pkt_ref, dqt_ref, dka_ref, dva_ref, dpka_ref, dpva_ref, pk_ref, pv_ref, lse_ref,
 ):
@@ -175,8 +140,8 @@
     segment = s_ref[0]
     pk_ref[...] = jnp.zeros_like(pk_ref)
     pv_ref[...] = jnp.zeros_like(pv_ref)
-    pk_ref[:SUMS] = pk_in[...]
-    pv_ref[:SUMS] = pv_in[...]
+    pk_ref[:SUMS] = prompt_ref[0]
+    pv_ref[:SUMS] = prompt_ref[1]
     kt_ref[...] = jnp.transpose(k_ref[...])
     pkt_ref[...] = jnp.transpose(pk_ref[...])
     for acc in (dka_ref, dva_ref, dpka_ref, dpva_ref):
@@ -236,10 +201,10 @@
     dp_ref[1] = dpva_ref[:SUMS].astype(BF)
 
 
-def backward(scalars, q, k, v, g, pk, pv, lses):
+def backward(scalars, q, k, v, g, prompts, lses):
     wide = 8 * HD
     rows = pl.BlockSpec((TOK, wide), lambda i, s: (0, i))
-    prompt = pl.BlockSpec((SUMS, wide), lambda i, s: (0, i))
+    prompt = pl.BlockSpec((2, SUMS, wide), lambda i, s: (0, 0, i))
     return pl.pallas_call(
         bwd_kernel,
         out_shape=(jax.ShapeDtypeStruct((TOK, WIDTH), BF),) * 3
@@ -247,8 +212,8 @@
         grid_spec=pltpu.PrefetchScalarGridSpec(
             num_scalar_prefetch=1,
             grid=(2,),
-            in_specs=[rows] * 4 + [prompt] * 2 + [pl.BlockSpec((4, TOK), lambda i, s: (0, 0))] * 4,
-            out_specs=(rows, rows, rows, pl.BlockSpec((2, SUMS, wide), lambda i, s: (0, 0, i))),
+            in_specs=[rows] * 4 + [prompt] + [pl.BlockSpec((4, TOK), lambda i, s: (0, 0))] * 4,
+            out_specs=(rows, rows, rows, prompt),
             scratch_shapes=[
                 pltpu.VMEM((wide, TOK), BF),
                 pltpu.VMEM((wide, PAD), BF),
@@ -267,7 +232,7 @@
             flops=16 * 5 * 2 * 896 * 256 * 256, transcendentals=16 * 896 * 256, bytes_accessed=10000000
         ),
         name="attend_back",
-    )(scalars, q, k, v, g, pk, pv, *lses)
+    )(scalars, q, k, v, g, prompts, *lses)
 
 
 WCOLS = 640
@@ -280,41 +245,58 @@
         quad = (s_ref[1] + by) & (SIDE - 1)
         for j in range(places):
 
-            @pl.when((pl.program_id(0) == 0) & (quad == s_ref[ORDER + j]))
+            @pl.when(quad == s_ref[ORDER + j])
             def _():
                 picked[n, 0] = owns[j][...]
                 picked[n, 1] = others[j][...]
 
     for n, out_ref in enumerate(outs):
-        out = dot(picked[n, 0], g_ref[...]) + dot(picked[n, 1], h_ref[...])
-        for sub in range(SIDE):
-            for tile in range(WCOLS // 128):
-                out_ref[sub, tile] = out[sub * SUB : sub * SUB + SUB, tile * 128 : tile * 128 + 128].astype(
-                    out_ref.dtype
-                )
+        for part in range(HALF // WCOLS):
+            w = pl.ds(pl.multiple_of(s_ref[0] * HALF + part * WCOLS, 128), WCOLS)
+            out = dot(picked[n, 0], g_ref[:, w]) + dot(picked[n, 1], h_ref[:, w])
+            for sub in range(SIDE):
+                for tile in range(WCOLS // 128):
+                    out_ref[sub, part * (WCOLS // 128) + tile] = out[
+                        sub * SUB : sub * SUB + SUB, tile * 128 : tile * 128 + 128
+                    ].astype(out_ref.dtype)
 
 
 def weight_quads(bys, scalars, owns, others, grad_rows, grad_other):
     count, places = len(bys), len(owns)
-    quad = pl.BlockSpec((QUAD, TOK), lambda n, s: (0, 0))
-    columns = pl.BlockSpec((TOK, WCOLS), lambda n, s: (0, n + s[0] * (HALF // WCOLS)))
+    vmem = pl.BlockSpec(memory_space=pltpu.VMEM)
     outs = pl.pallas_call(
         functools.partial(weight_kernel, bys, places),
         out_shape=[jax.ShapeDtypeStruct((SIDE, TILES, SUB, 128), BF if by else F32) for by in bys],
-        grid_spec=pltpu.PrefetchScalarGridSpec(
-            num_scalar_prefetch=1,
-            grid=(HALF // WCOLS,),
-            in_specs=[quad] * (2 * places) + [columns, columns],
-            out_specs=[pl.BlockSpec((SIDE, WCOLS // 128, SUB, 128), lambda n, s: (0, n, 0, 0))] * count,
-            scratch_shapes=[pltpu.VMEM((count, 2, QUAD, TOK), BF)],
-        ),
-        compiler_params=pltpu.CompilerParams(vmem_limit_bytes=24 << 20),
+        in_specs=[pl.BlockSpec(memory_space=pltpu.SMEM)] + [vmem] * (2 * places + 2),
+        out_specs=[vmem] * count,
+        scratch_shapes=[pltpu.VMEM((count, 2, QUAD, TOK), BF)],
+        compiler_params=pltpu.CompilerParams(vmem_limit_bytes=16 << 20),
         cost_estimate=pl.CostEstimate(
             flops=count * 4 * QUAD * TOK * HALF, transcendentals=0, bytes_accessed=4200000
         ),
         name="weight_quads",
     )(scalars, *owns, *others, grad_rows, grad_other)
     return [out.reshape(SIDE, PIECE, 128) for out in outs]
+
+
+def line_kernel(s_ref, own, r1, r2, r3, *outs):
+    for by, out in enumerate(outs):
+        n = (s_ref[2] + by) & (SIDE - 1)
+        total = (own[n] + r2[n].astype(F32)) + (r1[n].astype(F32) + r3[n].astype(F32))
+        out[...] = total.astype(out.dtype)
+
+
+def sum_line(scalars, own, r1, r2, r3):
+    vmem = pl.BlockSpec(memory_space=pltpu.VMEM)
+    return pl.pallas_call(
+        line_kernel,
+        out_shape=[jax.ShapeDtypeStruct((PIECE, 128), kind) for kind in (F32, BF, BF, BF)],
+        in_specs=[pl.BlockSpec(memory_space=pltpu.SMEM)] + [vmem] * 4,
+        out_specs=[vmem] * 4,
+        compiler_params=pltpu.CompilerParams(vmem_limit_bytes=8 << 20),
+        cost_estimate=pl.CostEstimate(flops=2000000, transcendentals=0, bytes_accessed=5000000),
+        name="sum_line",
+    )(scalars, own, r1, r2, r3)
 
 
 def order_kernel(s_ref, o_ref):
@@ -342,30 +324,6 @@
     )(where)
 
 
-def line_kernel(s_ref, own, r1, r2, r3, o0, o1, o2, o3):
-    total = (own[0] + r2[0].astype(F32)) + (r1[0].astype(F32) + r3[0].astype(F32))
-    for by, out in enumerate((o0, o1, o2, o3)):
-
-        @pl.when(pl.program_id(0) == by)
-        def _():
-            out[...] = total.astype(out.dtype)
-
-
-def sum_line(scalars, own, r1, r2, r3):
-    block = pl.BlockSpec((1, PIECE, 128), lambda n, s: ((s[2] + n) % SIDE, 0, 0))
-    whole = pl.BlockSpec((PIECE, 128), lambda n, s: (0, 0))
-    return pl.pallas_call(
-        line_kernel,
-        out_shape=[jax.ShapeDtypeStruct((PIECE, 128), kind) for kind in (F32, BF, BF, BF)],
-        grid_spec=pltpu.PrefetchScalarGridSpec(
-            num_scalar_prefetch=1, grid=(SIDE,), in_specs=[block] * 4, out_specs=[whole] * 4
-        ),
-        compiler_params=pltpu.CompilerParams(vmem_limit_bytes=16 << 20),
-        cost_estimate=pl.CostEstimate(flops=2000000, transcendentals=0, bytes_accessed=5000000),
-        name="sum_line",
-    )(scalars, own, r1, r2, r3)
-
-
 def mid_kernel(own, r1, r2, r3, out):
     total = (own[...] + r2[...].astype(F32)) + (r1[...].astype(F32) + r3[...].astype(F32))
     out[...] = total.astype(BF)
@@ -408,22 +366,17 @@
 
 def final_kernel(s_ref, *refs):
     pieces, later, out_hbm, dpk_hbm, dpv_hbm = refs[:8], refs[8], refs[9], refs[10], refs[11]
-    bufs, outs, sem, out_sem = refs[12:]
+    outs, out_sem = refs[12:]
     hand = [
         pltpu.make_async_copy(later.at[n], to, out_sem.at[8 + n]) for n, to in enumerate((dpk_hbm, dpv_hbm))
     ]
     for move in hand:
         move.start()
     segment, x, y, z = s_ref[0], s_ref[3], s_ref[4], s_ref[5]
-    moves = [pltpu.make_async_copy(pieces[n], bufs.at[n], sem.at[n]) for n in range(8)]
-    for move in moves:
-        move.start()
     total = jnp.zeros((1, 128), F32)
-    for n in range(8):
-        moves[n].wait()
+    for piece in pieces:
         for p in range(SIDE):
-            stat = bufs[n, p, PIECE : PIECE + STAT, :].astype(F32)
-            total = total + jnp.sum(stat, 0, keepdims=True)
+            total = total + jnp.sum(piece[p, PIECE : PIECE + STAT, :].astype(F32), 0, keepdims=True)
     mean = jnp.sum(total, 1, keepdims=True) * (1.0 / (WIDTH * D))
     scale = jnp.minimum(1.0, 1.0 / jnp.sqrt(mean + 1e-06))
     writes = []
@@ -436,7 +389,7 @@
             rows = pl.ds(pl.multiple_of((at + SIDE - p) % SIDE * SUB, 16), SUB)
             for tile in range(TILES):
                 outs[n, rows, tile * 128 : tile * 128 + 128] = (
-                    bufs[n, p, tile * SUB : tile * SUB + SUB, :].astype(F32) * scale
+                    pieces[n][p, tile * SUB : tile * SUB + SUB, :].astype(F32) * scale
                 ).astype(BF)
         write = pltpu.make_async_copy(
             outs.at[n],
@@ -452,23 +405,17 @@
 
 
 def finish(scalars, pieces, later):
-    any_spec = pl.BlockSpec(memory_space=pl.ANY)
+    vmem, any_spec = pl.BlockSpec(memory_space=pltpu.VMEM), pl.BlockSpec(memory_space=pl.ANY)
     return pl.pallas_call(
         final_kernel,
         out_shape=(jax.ShapeDtypeStruct((WIDTH, D), BF),) + (jax.ShapeDtypeStruct((SUMS, WIDTH), BF),) * 2,
-        grid_spec=pltpu.PrefetchScalarGridSpec(
-            num_scalar_prefetch=1,
-            grid=(1,),
-            in_specs=[any_spec] * 9,
-            out_specs=(any_spec,) * 3,
-            scratch_shapes=[
-                pltpu.VMEM((8, SIDE, PIECE + STAT, 128), BF),
-                pltpu.VMEM((8, QUAD, HALF), BF),
-                pltpu.SemaphoreType.DMA((8,)),
-                pltpu.SemaphoreType.DMA((10,)),
-            ],
-        ),
-        compiler_params=pltpu.CompilerParams(vmem_limit_bytes=32 << 20),
+        in_specs=[pl.BlockSpec(memory_space=pltpu.SMEM)] + [vmem] * 8 + [any_spec],
+        out_specs=(any_spec,) * 3,
+        scratch_shapes=[
+            pltpu.VMEM((8, QUAD, HALF), BF),
+            pltpu.SemaphoreType.DMA((10,)),
+        ],
+        compiler_params=pltpu.CompilerParams(vmem_limit_bytes=16 << 20),
         cost_estimate=pl.CostEstimate(flops=7000000, transcendentals=0, bytes_accessed=14000000),
         name="clip",
     )(scalars, *pieces, later)
@@ -497,16 +444,15 @@
     q, k, v, grad_rows = query_rows[0], key_rows[0], value_rows[0], out_grad[0]
     grad_other = lax.ppermute(grad_rows, "seg", SWAP)
     where = jnp.stack([lax.axis_index("seg"), lax.axis_index("dp")]).astype(jnp.int32)
-    scalars, prompt_keys, prompt_values = lax.optimization_barrier(
-        (order_scalars(where), prompt_keys, prompt_values)
+    scalars, prompts = lax.optimization_barrier(
+        (order_scalars(where), jnp.stack([prompt_keys[0], prompt_values[0]]))
     )
-    pk = lax.ppermute(prompt_keys[0], "seg", [(0, 1)])
-    pv = lax.ppermute(prompt_values[0], "seg", [(0, 1)])
+    prompts = lax.ppermute(prompts, "seg", [(0, 1)])
 
     attn, other, lses, sent = [], [], [], {}
 
     def forward(place, after=()):
-        out, lse = forward_quad(place, scalars, q, k, v, pk, pv, after)
+        out, lse = forward_quad(place, scalars, q, k, v, prompts, after)
         attn.append(out)
         lses.append(lse)
         other.append(lax.ppermute(out, "seg", SWAP))
@@ -532,11 +478,15 @@
     own = jnp.stack([own] + [lax.ppermute(own, BOTH, along("z", "x", by)) for by in (1, 2, 3)])
 
     own, head_low = lax.optimization_barrier((own, head_low))
-    pieces = [own] + [lax.ppermute(own, BOTH, along("x", "y", by)) for by in (1, 2, 3)]
-    dq, dk, dv, dp = backward(scalars, q, k, v, head_low, pk, pv, lses)
-    pieces, dp = lax.optimization_barrier((pieces, dp))
-    pieces = pieces + [lax.ppermute(part, "seg", SWAP) for part in pieces]
-    weight_grad, dpk, dpv = finish(scalars, pieces, lax.ppermute(dp, "seg", [(1, 0)]))
+    pieces = [lax.ppermute(own, BOTH, along("x", "y", by)) for by in (1, 2, 3)]
+    dq, dk, dv, dp = backward(scalars, q, k, v, head_low, prompts, lses)
+    own, dp = lax.optimization_barrier((own, dp))
+    later = lax.ppermute(dp, "seg", [(1, 0)])
+    swapped = [lax.ppermute(own, "seg", SWAP)]
+    for n in range(3):
+        pieces[n], _ = lax.optimization_barrier((pieces[n], dp))
+        swapped.append(lax.ppermute(pieces[n], "seg", SWAP))
+    weight_grad, dpk, dpv = finish(scalars, [own] + pieces + swapped, later)
     return (dq[None], dk[None], dv[None], dpk[None], dpv[None], weight_grad)
 
 

time: 122 us -> 118 us (0.967)
  Pallas kernels: 43.8 us -> 39.9 us
  waiting for transfers between devices: 38.3 us -> 34.4 us
  starting transfers between devices: 34.7 us -> 37.3 us
    ppermute x10 -> x9, waiting for transfers between devices: 9.56 us -> 4.5 us  [the longest x1 2.32 us: program(): later = lax.ppermute(dp, 'seg', [(1, 0)])]
    ppermute x10 -> x9, starting transfers between devices: 14.2 us -> 16.9 us  [the longest x1 5.57 us: program(): swapped = [lax.ppermute(own, 'seg', SWAP)]]
    pallas_call x3, Pallas kernels: 8.24 us -> 6.51 us  [weight_quads(): pl.pallas_call(functools.partial(weight_kernel, bys, places), out_shape=[...]
  transfers between devices with their start and end apart: 27 -> 26, of which waited for: 16 -> 13; matrix products, arithmetic and copies ran while one was open for 3% -> 4% of each run, Pallas kernels for 24% -> 24%
where the time goes in v1:
time: 118 us; the launch traced here: 117 us
  Pallas kernels  39.9 us (34%)
  starting transfers between devices  37.3 us (32%)
  waiting for transfers between devices  34.4 us (29%)
  matrix products  3.59 us (3%)
  other arithmetic  1.19 us (1%)
    pallas_call x1, Pallas kernels, backward(): pl.pallas_call(bwd_kernel, out_shape=(jax.ShapeDtypeStruct((TOK, WIDTH),...  16.6 us
    pallas_call x4, Pallas kernels, forward_quad(): pl.pallas_call(functools.partial(fwd_kernel, place), out_shape=(jax.Shape...  10.8 us
    ppermute x3, waiting for transfers between devices, send(): sent[by] = lax.ppermute(part, BOTH, along('x', 'y', by)) if by else part  9.17 us
    ppermute x3, waiting for transfers between devices, program(): lax.ppermute(own, BOTH, along('y', 'z', by))  7.6 us
    ppermute x3, waiting for transfers between devices, program(): lax.ppermute(own, BOTH, along('z', 'x', by))  7.38 us
    pallas_call x3, Pallas kernels, weight_quads(): pl.pallas_call(functools.partial(weight_kernel, bys, places), out_shape=[...  6.51 us
    ppermute x1, starting transfers between devices, program(): swapped = [lax.ppermute(own, 'seg', SWAP)]  5.57 us
    ppermute x3, starting transfers between devices, program(): swapped.append(lax.ppermute(pieces[n], 'seg', SWAP))  4.97 us
  transfers between devices with their start and end apart: 26, of which 13 were waited for; matrix products, arithmetic and copies ran while one was open for 4% of the time, Pallas kernels for 24%

profile of v1, /device:TPU:1, one launch (start us, length us, event | category | flops | bytes accessed | tf_op | source)
XLA Modules:
  0.0 117.5 jit_solution(7943684785640493345)
XLA Ops:
  0.6 1.5 %collective-permute-start.3 = (bf16[512,2560]{1,0:T(8,128)(2,1)}, bf16[512,2560]{1,0:T(8,128)(2,1)S(1)}, u32[]{:S(2)}, u32[]{:S(2)}) collective-permute-start(bf16[512,2560]{1,0:T(8,128)(2,1)} %bitcast.22), channel_id=1, source_target_pairs={{0,64},{64,0},{1,65},{65,1},{2,66},{66,2},{3,67},{67,3},{4,68},{68... | collective-permute-start | bytes 7864328 | tf_op jit(solution)/shard_map/ppermute | solution.py:445
  2.1 0.1 pad_add_fusion.s_ref
  2.2 1.0 pad_maximum_fusion.1
  3.2 0.0 copy-start.1
  3.2 0.0 copy-start.2
  3.2 0.0 copy-start.3
  3.2 1.1 order.1.s_ref
  4.4 1.3 %collective-permute-start = (bf16[2,50,1280]{2,1,0:T(8,128)(2,1)S(1)}, bf16[2,50,1280]{2,1,0:T(8,128)(2,1)S(1)}, u32[]{:S(2)}, u32[]{:S(2)}) collective-permute-start(bf16[2,50,1280]{2,1,0:T(8,128)(2,1)S(1)} %pad_maximum_fusion.1), channel_id=1, source_target_pairs={{0,64},{1,65},{2,66},{3,67},{4,68},{5,69},{6,70},{7,71},{8,72},{9,... | collective-permute-start | bytes 768008 | tf_op jit(solution)/shard_map/ppermute | solution.py:450
  5.7 2.2 %collective-permute-done.prompt_ref = bf16[2,50,1280]{2,1,0:T(8,128)(2,1)S(1)} collective-permute-done((bf16[2,50,1280]{2,1,0:T(8,128)(2,1)S(1)}, bf16[2,50,1280]{2,1,0:T(8,128)(2,1)S(1)}, u32[]{:S(2)}, u32[]{:S(2)}) %collective-permute-start) | collective-permute-done | bytes 256032 | tf_op jit(solution)/shard_map/ppermute | solution.py:450
  7.8 2.7 %fwd_quad.4 = (bf16[320,512]{1,0:T(8,128)(2,1)S(1)}, f32[4,512]{1,0:T(4,128)S(1)}) custom-call(s32[10]{0:T(128)S(1)} %order.1.s_ref, bf16[512,1280]{1,0:T(8,128)(2,1)S(1)} %bitcast.26, bf16[512,1280]{1,0:T(8,128)(2,1)S(1)} %bitcast.31, bf16[512,1280]{1,0:T(8,128)(2,1)S(1)} %bitcast.36, bf16[2,50,1280]{2,1,0:T(8,128)(2,1)S(1)} %collective-permute-done.prompt_ref), custom_call_target="tpu_custom_call" | custom-call | flops 939524096 | bytes 1600000 | tf_op jit(solution)/shard_map/fwd_quad/pallas_call | solution.py:110
  10.5 0.0 copy-start
  10.5 2.7 %fwd_quad.5 = (bf16[320,512]{1,0:T(8,128)(2,1)S(1)}, f32[4,512]{1,0:T(4,128)S(1)}) custom-call(s32[10]{0:T(128)S(1)} %order.1.s_ref, bf16[512,1280]{1,0:T(8,128)(2,1)S(1)} %bitcast.27, bf16[512,1280]{1,0:T(8,128)(2,1)S(1)} %bitcast.32, bf16[512,1280]{1,0:T(8,128)(2,1)S(1)} %bitcast.37, bf16[2,50,1280]{2,1,0:T(8,128)(2,1)S(1)} %collective-permute-done.prompt_ref, ...), custom_call_target="tpu_custom_call" | custom-call | flops 939524096 | bytes 1600000 | tf_op jit(solution)/shard_map/fwd_quad/pallas_call | solution.py:110
  13.2 0.2 collective-permute-start.2
  13.5 0.4 collective-permute-start.1
  13.8 1.1 collective-permute-done.2.refs_3_.refs_5_
  15.0 0.5 collective-permute-done.1.refs_2_.refs_4_
  15.4 1.8 %weight_quads.3 = bf16[4,10,80,128]{3,2,1,0:T(8,128)(2,1)S(1)} custom-call(s32[10]{0:T(128)S(1)} %order.1.s_ref, bf16[320,512]{1,0:T(8,128)(2,1)S(1)} %get-tuple-element.43.rest_0_.refs_0_, bf16[320,512]{1,0:T(8,128)(2,1)S(1)} %get-tuple-element.44.refs_1_, bf16[320,512]{1,0:T(8,128)(2,1)S(1)} %collective-permute-done.1.refs_2_.refs_4_, ...), custom_call_target="tpu_custom_call" | custom-call | flops 838860800 | bytes 4200000 | tf_op jit(solution)/shard_map/weight_quads/pallas_call | solution.py:267
  17.2 2.7 %fwd_quad.6 = (bf16[320,512]{1,0:T(8,128)(2,1)S(1)}, f32[4,512]{1,0:T(4,128)S(1)}) custom-call(s32[10]{0:T(128)S(1)} %order.1.s_ref, bf16[512,1280]{1,0:T(8,128)(2,1)S(1)} %bitcast.28, bf16[512,1280]{1,0:T(8,128)(2,1)S(1)} %bitcast.33, bf16[512,1280]{1,0:T(8,128)(2,1)S(1)} %bitcast.38, bf16[2,50,1280]{2,1,0:T(8,128)(2,1)S(1)} %collective-permute-done.prompt_ref, ...), custom_call_target="tpu_custom_call" | custom-call | flops 939524096 | bytes 1600000 | tf_op jit(solution)/shard_map/fwd_quad/pallas_call | solution.py:110
  19.9 0.0 slice-start
  19.9 2.7 %fwd_quad.7 = (bf16[320,512]{1,0:T(8,128)(2,1)S(1)}, f32[4,512]{1,0:T(4,128)S(1)}) custom-call(s32[10]{0:T(128)S(1)} %order.1.s_ref, bf16[512,1280]{1,0:T(8,128)(2,1)S(1)} %bitcast.29, bf16[512,1280]{1,0:T(8,128)(2,1)S(1)} %bitcast.34, bf16[512,1280]{1,0:T(8,128)(2,1)S(1)} %bitcast.39, bf16[2,50,1280]{2,1,0:T(8,128)(2,1)S(1)} %collective-permute-done.prompt_ref, ...), custom_call_target="tpu_custom_call" | custom-call | flops 939524096 | bytes 1600000 | tf_op jit(solution)/shard_map/fwd_quad/pallas_call | solution.py:110
  22.7 0.0 slice-start.1
  22.7 0.2 collective-permute-start.5
  22.9 0.4 collective-permute-start.4
  23.3 3.0 %collective-permute-start.7 = (bf16[4,800,128]{2,1,0:T(8,128)(2,1)S(1)}, bf16[4,800,128]{2,1,0:T(8,128)(2,1)S(1)}, u32[]{:S(2)}, u32[]{:S(2)}) collective-permute-start(bf16[4,800,128]{2,1,0:T(8,128)(2,1)S(1)} %bitcast.43), channel_id=1, source_target_pairs={{0,2},{1,3},{2,0},{3,1},{4,6},{5,7},{6,4},{7,5},{8,10},{9,11},{10,... | collective-permute-start | bytes 2457608 | tf_op jit(solution)/shard_map/ppermute | solution.py:463
  26.3 2.9 %weight_quads.5 = (bf16[4,10,80,128]{3,2,1,0:T(8,128)(2,1)S(1)}, bf16[4,10,80,128]{3,2,1,0:T(8,128)(2,1)S(1)}) custom-call(s32[10]{0:T(128)S(1)} %order.1.s_ref, bf16[320,512]{1,0:T(8,128)(2,1)S(1)} %get-tuple-element.43.rest_0_.refs_0_, bf16[320,512]{1,0:T(8,128)(2,1)S(1)} %get-tuple-element.44.refs_1_, ...), custom_call_target="tpu_custom_call" | custom-call | flops 1677721600 | bytes 4200000 | tf_op jit(solution)/shard_map/weight_quads/pallas_call | solution.py:267
  29.2 1.6 %collective-permute-start.8 = (bf16[4,800,128]{2,1,0:T(8,128)(2,1)S(1)}, bf16[4,800,128]{2,1,0:T(8,128)(2,1)S(1)}, u32[]{:S(2)}, u32[]{:S(2)}) collective-permute-start(bf16[4,800,128]{2,1,0:T(8,128)(2,1)S(1)} %bitcast.47), channel_id=1, source_target_pairs={{0,3},{1,0},{2,1},{3,2},{4,7},{5,4},{6,5},{7,6},{8,11},{9,8},{10,9... | collective-permute-start | bytes 2457608 | tf_op jit(solution)/shard_map/ppermute | solution.py:463
  30.9 0.1 collective-permute-start.6
  30.9 3.6 %convolution_convert_fusion.g_ref = bf16[512,1280]{1,0:T(8,128)(2,1)S(1)} fusion(bf16[1280,2560]{1,0:T(8,128)(2,1)S(1)} %bitcast.52, bf16[1,512,2560]{2,1,0:T(8,128)(2,1)S(1)} %copy-done), kind=kOutput, calls=%fused_computation | convolution fusion | flops 3356098560 | bytes 10485760 | tf_op jit(solution)/shard_map/td,hd->th/dot_general | solution.py:473
  34.5 1.8 %weight_quads.4 = f32[4,10,80,128]{3,2,1,0:T(8,128)S(1)} custom-call(s32[10]{0:T(128)S(1)} %order.1.s_ref, bf16[320,512]{1,0:T(8,128)(2,1)S(1)} %get-tuple-element.43.rest_0_.refs_0_, bf16[320,512]{1,0:T(8,128)(2,1)S(1)} %get-tuple-element.44.refs_1_, bf16[320,512]{1,0:T(8,128)(2,1)S(1)} %get-tuple-element.45.rest_1_.refs_2_, ...), custom_call_target="tpu_custom_call" | custom-call | flops 838860800 | bytes 4200000 | tf_op jit(solution)/shard_map/weight_quads/pallas_call | solution.py:267
  36.4 9.2 %collective-permute-done.8.r3 = bf16[4,800,128]{2,1,0:T(8,128)(2,1)S(1)} collective-permute-done((bf16[4,800,128]{2,1,0:T(8,128)(2,1)S(1)}, bf16[4,800,128]{2,1,0:T(8,128)(2,1)S(1)}, u32[]{:S(2)}, u32[]{:S(2)}) %collective-permute-start.8) | collective-permute-done | bytes 819232 | tf_op jit(solution)/shard_map/ppermute | solution.py:463
  45.5 0.9 sum_line.1
  46.5 1.3 %collective-permute-start.9 = (bf16[800,128]{1,0:T(8,128)(2,1)S(1)}, bf16[800,128]{1,0:T(8,128)(2,1)S(1)}, u32[]{:S(2)}, u32[]{:S(2)}) collective-permute-start(bf16[800,128]{1,0:T(8,128)(2,1)S(1)} %get-tuple-element.54), channel_id=1, source_target_pairs={{0,16},{1,17},{2,18},{3,19},{4,20},{5,21},{6,22},{7,23},{8,24},{9,... | collective-permute-start | bytes 614408 | tf_op jit(solution)/shard_map/ppermute | solution.py:476
  47.7 2.5 %collective-permute-start.10 = (bf16[800,128]{1,0:T(8,128)(2,1)S(1)}, bf16[800,128]{1,0:T(8,128)(2,1)S(1)}, u32[]{:S(2)}, u32[]{:S(2)}) collective-permute-start(bf16[800,128]{1,0:T(8,128)(2,1)S(1)} %get-tuple-element.55), channel_id=1, source_target_pairs={{0,32},{1,33},{2,34},{3,35},{4,36},{5,37},{6,38},{7,39},{8,40},{9,... | collective-permute-start | bytes 614408 | tf_op jit(solution)/shard_map/ppermute | solution.py:476
  50.2 1.1 collective-permute-start.11
  51.3 1.3 %collective-permute-done.9.r1 = bf16[800,128]{1,0:T(8,128)(2,1)S(1)} collective-permute-done((bf16[800,128]{1,0:T(8,128)(2,1)S(1)}, bf16[800,128]{1,0:T(8,128)(2,1)S(1)}, u32[]{:S(2)}, u32[]{:S(2)}) %collective-permute-start.9) | collective-permute-done | bytes 204832 | tf_op jit(solution)/shard_map/ppermute | solution.py:476
  52.6 2.9 %collective-permute-done.10.r2 = bf16[800,128]{1,0:T(8,128)(2,1)S(1)} collective-permute-done((bf16[800,128]{1,0:T(8,128)(2,1)S(1)}, bf16[800,128]{1,0:T(8,128)(2,1)S(1)}, u32[]{:S(2)}, u32[]{:S(2)}) %collective-permute-start.10) | collective-permute-done | bytes 204832 | tf_op jit(solution)/shard_map/ppermute | solution.py:476
  55.5 0.1 sum_mid.1.own
  55.7 3.8 %collective-permute-start.14 = (bf16[800,128]{1,0:T(8,128)(2,1)S(1)}, bf16[800,128]{1,0:T(8,128)(2,1)S(1)}, u32[]{:S(2)}, u32[]{:S(2)}) collective-permute-start(bf16[800,128]{1,0:T(8,128)(2,1)S(1)} %sum_mid.1.own), channel_id=1, source_target_pairs={{0,12},{1,13},{2,14},{3,15},{4,0},{5,1},{6,2},{7,3},{8,4},{9,5},{1... | collective-permute-start | bytes 614408 | tf_op jit(solution)/shard_map/ppermute | solution.py:477
  59.5 0.0 collective-permute-start.13
  59.5 0.7 collective-permute-start.12
  60.2 4.2 %collective-permute-done.14.r3 = bf16[800,128]{1,0:T(8,128)(2,1)S(1)} collective-permute-done((bf16[800,128]{1,0:T(8,128)(2,1)S(1)}, bf16[800,128]{1,0:T(8,128)(2,1)S(1)}, u32[]{:S(2)}, u32[]{:S(2)}) %collective-permute-start.14) | collective-permute-done | bytes 204832 | tf_op jit(solution)/shard_map/ppermute | solution.py:477
  64.4 1.3 %collective-permute-done.13.r2 = bf16[800,128]{1,0:T(8,128)(2,1)S(1)} collective-permute-done((bf16[800,128]{1,0:T(8,128)(2,1)S(1)}, bf16[800,128]{1,0:T(8,128)(2,1)S(1)}, u32[]{:S(2)}, u32[]{:S(2)}) %collective-permute-start.13) | collective-permute-done | bytes 204832 | tf_op jit(solution)/shard_map/ppermute | solution.py:477
  65.7 2.1 %collective-permute-done.12.r1 = bf16[800,128]{1,0:T(8,128)(2,1)S(1)} collective-permute-done((bf16[800,128]{1,0:T(8,128)(2,1)S(1)}, bf16[800,128]{1,0:T(8,128)(2,1)S(1)}, u32[]{:S(2)}, u32[]{:S(2)}) %collective-permute-start.12) | collective-permute-done | bytes 204832 | tf_op jit(solution)/shard_map/ppermute | solution.py:477
  67.8 0.1 sum_cross.1
  67.9 2.3 %collective-permute-start.17 = (bf16[808,128]{1,0:T(8,128)(2,1)S(1)}, bf16[808,128]{1,0:T(8,128)(2,1)S(1)}, u32[]{:S(2)}, u32[]{:S(2)}) collective-permute-start(bf16[808,128]{1,0:T(8,128)(2,1)S(1)} %sum_cross.1), channel_id=1, source_target_pairs={{0,48},{1,49},{2,50},{3,51},{4,52},{5,53},{6,54},{7,55},{8,56},{9,... | collective-permute-start | bytes 620552 | tf_op jit(solution)/shard_map/ppermute | solution.py:478
  70.3 0.9 collective-permute-start.16
  71.1 0.4 collective-permute-start.15
  71.5 3.7 %collective-permute-done.17 = bf16[808,128]{1,0:T(8,128)(2,1)S(1)} collective-permute-done((bf16[808,128]{1,0:T(8,128)(2,1)S(1)}, bf16[808,128]{1,0:T(8,128)(2,1)S(1)}, u32[]{:S(2)}, u32[]{:S(2)}) %collective-permute-start.17) | collective-permute-done | bytes 206880 | tf_op jit(solution)/shard_map/ppermute | solution.py:478
  75.2 1.3 %collective-permute-done.16 = bf16[808,128]{1,0:T(8,128)(2,1)S(1)} collective-permute-done((bf16[808,128]{1,0:T(8,128)(2,1)S(1)}, bf16[808,128]{1,0:T(8,128)(2,1)S(1)}, u32[]{:S(2)}, u32[]{:S(2)}) %collective-permute-start.16) | collective-permute-done | bytes 206880 | tf_op jit(solution)/shard_map/ppermute | solution.py:478
  76.5 2.4 %collective-permute-done.15 = bf16[808,128]{1,0:T(8,128)(2,1)S(1)} collective-permute-done((bf16[808,128]{1,0:T(8,128)(2,1)S(1)}, bf16[808,128]{1,0:T(8,128)(2,1)S(1)}, u32[]{:S(2)}, u32[]{:S(2)}) %collective-permute-start.15) | collective-permute-done | bytes 206880 | tf_op jit(solution)/shard_map/ppermute | solution.py:478
  78.9 0.1 pad_maximum_fusion.refs_0_
  79.0 2.4 %collective-permute-start.20 = (bf16[4,808,128]{2,1,0:T(8,128)(2,1)S(1)}, bf16[4,808,128]{2,1,0:T(8,128)(2,1)S(1)}, u32[]{:S(2)}, u32[]{:S(2)}) collective-permute-start(bf16[4,808,128]{2,1,0:T(8,128)(2,1)S(1)} %pad_maximum_fusion.refs_0_), channel_id=1, source_target_pairs={{0,3},{1,0},{2,1},{3,2},{4,7},{5,4},{6,5},{7,6},{8,11},{9,8},{10,9... | collective-permute-start | bytes 2482184 | tf_op jit(solution)/shard_map/ppermute | solution.py:481
  81.5 0.3 collective-permute-start.19
  81.8 0.4 collective-permute-start.18
  82.2 16.6 %attend_back.1 = (bf16[512,1280]{1,0:T(8,128)(2,1)}, bf16[512,1280]{1,0:T(8,128)(2,1)}, bf16[512,1280]{1,0:T(8,128)(2,1)}, bf16[2,50,1280]{2,1,0:T(8,128)(2,1)S(1)}) custom-call(s32[10]{0:T(128)S(1)} %order.1.s_ref, bf16[512,1280]{1,0:T(8,128)(2,1)S(1)} %bitcast.30, bf16[512,1280]{1,0:T(8,128)(2,1)S(1)} %bitcast.35, bf16[512,1280]{1,0:T(8,128)(2,1)S(1)} %bitcast.40, ...), custom_call_target="tpu_custom_call" | custom-call | flops 9395240960 | bytes 10000000 | tf_op jit(solution)/shard_map/attend_back/pallas_call | solution.py:208
  98.8 5.6 %collective-permute-start.21 = (bf16[4,808,128]{2,1,0:T(8,128)(2,1)S(1)}, bf16[4,808,128]{2,1,0:T(8,128)(2,1)S(1)}, u32[]{:S(2)}, u32[]{:S(2)}) collective-permute-start(bf16[4,808,128]{2,1,0:T(8,128)(2,1)S(1)} %pad_maximum_fusion.refs_0_), channel_id=1, source_target_pairs={{0,64},{64,0},{1,65},{65,1},{2,66},{66,2},{3,67},{67,3},{4,68},{68... | collective-permute-start | bytes 2482184 | tf_op jit(solution)/shard_map/ppermute | solution.py:485
  104.4 0.0 collective-permute-done.20.refs_3_
  104.4 0.0 collective-permute-done.19.refs_2_
  104.4 4.5 %collective-permute-start.22 = (bf16[4,808,128]{2,1,0:T(8,128)(2,1)S(1)}, bf16[4,808,128]{2,1,0:T(8,128)(2,1)S(1)}, u32[]{:S(2)}, u32[]{:S(2)}) collective-permute-start(bf16[4,808,128]{2,1,0:T(8,128)(2,1)S(1)} %collective-permute-done.18.refs_1_), channel_id=1, source_target_pairs={{0,64},{64,0},{1,65},{65,1},{2,66},{66,2},{3,67},{67,3},{4,68},{68... | collective-permute-start | bytes 2482184 | tf_op jit(solution)/shard_map/ppermute | solution.py:488
  108.8 0.0 collective-permute-start.23
  108.8 0.5 collective-permute-start.24
  109.4 1.9 %collective-permute-start.25 = (bf16[2,50,1280]{2,1,0:T(8,128)(2,1)S(1)}, bf16[2,50,1280]{2,1,0:T(8,128)(2,1)S(1)}, u32[]{:S(2)}, u32[]{:S(2)}) collective-permute-start(bf16[2,50,1280]{2,1,0:T(8,128)(2,1)S(1)} %get-tuple-element.69), channel_id=1, source_target_pairs={{64,0},{65,1},{66,2},{67,3},{68,4},{69,5},{70,6},{71,7},{72,8},{73... | collective-permute-start | bytes 768008 | tf_op jit(solution)/shard_map/ppermute | solution.py:484
  111.3 2.3 %collective-permute-done.25.refs_8_ = bf16[2,50,1280]{2,1,0:T(8,128)(2,1)S(1)} collective-permute-done((bf16[2,50,1280]{2,1,0:T(8,128)(2,1)S(1)}, bf16[2,50,1280]{2,1,0:T(8,128)(2,1)S(1)}, u32[]{:S(2)}, u32[]{:S(2)}) %collective-permute-start.25) | collective-permute-done | bytes 256032 | tf_op jit(solution)/shard_map/ppermute | solution.py:484
  113.6 3.7 %clip.1 = (bf16[1280,2560]{1,0:T(8,128)(2,1)}, bf16[50,1280]{1,0:T(8,128)(2,1)}, bf16[50,1280]{1,0:T(8,128)(2,1)}) custom-call(s32[10]{0:T(128)S(1)} %order.1.s_ref, bf16[4,808,128]{2,1,0:T(8,128)(2,1)S(1)} %pad_maximum_fusion.refs_0_, bf16[4,808,128]{2,1,0:T(8,128)(2,1)S(1)} %collective-permute-done.18.refs_1_, ...), custom_call_target="tpu_custom_call" | custom-call | flops 7000000 | bytes 14000000 | tf_op jit(solution)/shard_map/clip/pallas_call | solution.py:409
  (18 shorter events, 0.0 us)
Async XLA Ops:
  0.6 14.8 %collective-permute-start.3 = (bf16[512,2560]{1,0:T(8,128)(2,1)}, bf16[512,2560]{1,0:T(8,128)(2,1)S(1)}, u32[]{:S(2)}, u32[]{:S(2)}) collective-permute-start(bf16[512,2560]{1,0:T(8,128)(2,1)} %bitcast.22), channel_id=1, source_target_pairs={{0,64},{64,0},{1,65},{65,1},{2,66},{66,2},{3,67},{67,3},{4,68},{68... | collective-permute-start | bytes 7864328 | tf_op jit(solution)/shard_map/ppermute | solution.py:445
  3.2 4.7 %copy-start.1 = (bf16[1,512,1280]{2,1,0:T(8,128)(2,1)S(1)}, bf16[1,512,1280]{2,1,0:T(8,128)(2,1)}, u32[]{:S(2)}) copy-start(bf16[1,512,1280]{2,1,0:T(8,128)(2,1)} %param.7) | copy-start | bytes 3932164
  3.2 4.6 %copy-start.2 = (bf16[1,512,1280]{2,1,0:T(8,128)(2,1)S(1)}, bf16[1,512,1280]{2,1,0:T(8,128)(2,1)}, u32[]{:S(2)}) copy-start(bf16[1,512,1280]{2,1,0:T(8,128)(2,1)} %param.8) | copy-start | bytes 3932164
  3.2 4.6 %copy-start.3 = (bf16[1,512,1280]{2,1,0:T(8,128)(2,1)S(1)}, bf16[1,512,1280]{2,1,0:T(8,128)(2,1)}, u32[]{:S(2)}) copy-start(bf16[1,512,1280]{2,1,0:T(8,128)(2,1)} %param.9) | copy-start | bytes 3932164
  4.4 3.5 %collective-permute-start = (bf16[2,50,1280]{2,1,0:T(8,128)(2,1)S(1)}, bf16[2,50,1280]{2,1,0:T(8,128)(2,1)S(1)}, u32[]{:S(2)}, u32[]{:S(2)}) collective-permute-start(bf16[2,50,1280]{2,1,0:T(8,128)(2,1)S(1)} %pad_maximum_fusion.1), channel_id=1, source_target_pairs={{0,64},{1,65},{2,66},{3,67},{4,68},{5,69},{6,70},{7,71},{8,72},{9,... | collective-permute-start | bytes 768008 | tf_op jit(solution)/shard_map/ppermute | solution.py:450
  10.5 4.9 %copy-start = (bf16[1,512,2560]{2,1,0:T(8,128)(2,1)S(1)}, bf16[1,512,2560]{2,1,0:T(8,128)(2,1)}, u32[]{:S(2)}) copy-start(bf16[1,512,2560]{2,1,0:T(8,128)(2,1)} %param.12) | copy-start | bytes 7864324
  13.2 1.7 %collective-permute-start.2 = (bf16[320,512]{1,0:T(8,128)(2,1)S(1)}, bf16[320,512]{1,0:T(8,128)(2,1)S(1)}, u32[]{:S(2)}, u32[]{:S(2)}) collective-permute-start(bf16[320,512]{1,0:T(8,128)(2,1)S(1)} %get-tuple-element.44.refs_1_), channel_id=1, source_target_pairs={{0,64},{64,0},{1,65},{65,1},{2,66},{66,2},{3,67},{67,3},{4,68},{68... | collective-permute-start | bytes 983048 | tf_op jit(solution)/shard_map/ppermute | solution.py:458
  13.5 2.0 %collective-permute-start.1 = (bf16[320,512]{1,0:T(8,128)(2,1)S(1)}, bf16[320,512]{1,0:T(8,128)(2,1)S(1)}, u32[]{:S(2)}, u32[]{:S(2)}) collective-permute-start(bf16[320,512]{1,0:T(8,128)(2,1)S(1)} %get-tuple-element.43.rest_0_.refs_0_), channel_id=1, source_target_pairs={{0,64},{64,0},{1,65},{65,1},{2,66},{66,2},{3,67},{67,3},{4,68},{68... | collective-permute-start | bytes 983048 | tf_op jit(solution)/shard_map/ppermute | solution.py:458
  19.9 11.0 %slice-start = ((s8[6553600]{0:T(1024)(128)(4,1)}), s8[4194304]{0:T(1024)(128)(4,1)S(1)}, s32[]{:S(2)}) async-start(s8[6553600]{0:T(1024)(128)(4,1)} %bitcast.51), calls=%async_computation | async-start | bytes 8388608
  22.7 8.3 %slice-start.1 = ((s8[6553600]{0:T(1024)(128)(4,1)}), s8[2359296]{0:T(1024)(128)(4,1)S(1)}, s32[]{:S(2)}) async-start(s8[6553600]{0:T(1024)(128)(4,1)} %bitcast.51), calls=%async_computation.1 | async-start | bytes 4718592
  22.7 3.6 %collective-permute-start.5 = (bf16[320,512]{1,0:T(8,128)(2,1)S(1)}, bf16[320,512]{1,0:T(8,128)(2,1)S(1)}, u32[]{:S(2)}, u32[]{:S(2)}) collective-permute-start(bf16[320,512]{1,0:T(8,128)(2,1)S(1)} %get-tuple-element.46.refs_3_), channel_id=1, source_target_pairs={{0,64},{64,0},{1,65},{65,1},{2,66},{66,2},{3,67},{67,3},{4,68},{68... | collective-permute-start | bytes 983048 | tf_op jit(solution)/shard_map/ppermute | solution.py:458
  22.9 3.4 %collective-permute-start.4 = (bf16[320,512]{1,0:T(8,128)(2,1)S(1)}, bf16[320,512]{1,0:T(8,128)(2,1)S(1)}, u32[]{:S(2)}, u32[]{:S(2)}) collective-permute-start(bf16[320,512]{1,0:T(8,128)(2,1)S(1)} %get-tuple-element.45.rest_1_.refs_2_), channel_id=1, source_target_pairs={{0,64},{64,0},{1,65},{65,1},{2,66},{66,2},{3,67},{67,3},{4,68},{68... | collective-permute-start | bytes 983048 | tf_op jit(solution)/shard_map/ppermute | solution.py:458
  23.3 13.1 %collective-permute-start.7 = (bf16[4,800,128]{2,1,0:T(8,128)(2,1)S(1)}, bf16[4,800,128]{2,1,0:T(8,128)(2,1)S(1)}, u32[]{:S(2)}, u32[]{:S(2)}) collective-permute-start(bf16[4,800,128]{2,1,0:T(8,128)(2,1)S(1)} %bitcast.43), channel_id=1, source_target_pairs={{0,2},{1,3},{2,0},{3,1},{4,6},{5,7},{6,4},{7,5},{8,10},{9,11},{10,... | collective-permute-start | bytes 2457608 | tf_op jit(solution)/shard_map/ppermute | solution.py:463
  29.2 16.3 %collective-permute-start.8 = (bf16[4,800,128]{2,1,0:T(8,128)(2,1)S(1)}, bf16[4,800,128]{2,1,0:T(8,128)(2,1)S(1)}, u32[]{:S(2)}, u32[]{:S(2)}) collective-permute-start(bf16[4,800,128]{2,1,0:T(8,128)(2,1)S(1)} %bitcast.47), channel_id=1, source_target_pairs={{0,3},{1,0},{2,1},{3,2},{4,7},{5,4},{6,5},{7,6},{8,11},{9,8},{10,9... | collective-permute-start | bytes 2457608 | tf_op jit(solution)/shard_map/ppermute | solution.py:463
  30.9 14.7 %collective-permute-start.6 = (bf16[4,800,128]{2,1,0:T(8,128)(2,1)S(1)}, bf16[4,800,128]{2,1,0:T(8,128)(2,1)S(1)}, u32[]{:S(2)}, u32[]{:S(2)}) collective-permute-start(bf16[4,800,128]{2,1,0:T(8,128)(2,1)S(1)} %bitcast.46), channel_id=1, source_target_pairs={{0,1},{1,2},{2,3},{3,0},{4,5},{5,6},{6,7},{7,4},{8,9},{9,10},{10,1... | collective-permute-start | bytes 2457608 | tf_op jit(solution)/shard_map/ppermute | solution.py:463
  46.5 6.2 %collective-permute-start.9 = (bf16[800,128]{1,0:T(8,128)(2,1)S(1)}, bf16[800,128]{1,0:T(8,128)(2,1)S(1)}, u32[]{:S(2)}, u32[]{:S(2)}) collective-permute-start(bf16[800,128]{1,0:T(8,128)(2,1)S(1)} %get-tuple-element.54), channel_id=1, source_target_pairs={{0,16},{1,17},{2,18},{3,19},{4,20},{5,21},{6,22},{7,23},{8,24},{9,... | collective-permute-start | bytes 614408 | tf_op jit(solution)/shard_map/ppermute | solution.py:476
  47.7 7.8 %collective-permute-start.10 = (bf16[800,128]{1,0:T(8,128)(2,1)S(1)}, bf16[800,128]{1,0:T(8,128)(2,1)S(1)}, u32[]{:S(2)}, u32[]{:S(2)}) collective-permute-start(bf16[800,128]{1,0:T(8,128)(2,1)S(1)} %get-tuple-element.55), channel_id=1, source_target_pairs={{0,32},{1,33},{2,34},{3,35},{4,36},{5,37},{6,38},{7,39},{8,40},{9,... | collective-permute-start | bytes 614408 | tf_op jit(solution)/shard_map/ppermute | solution.py:476
  50.2 5.3 %collective-permute-start.11 = (bf16[800,128]{1,0:T(8,128)(2,1)S(1)}, bf16[800,128]{1,0:T(8,128)(2,1)S(1)}, u32[]{:S(2)}, u32[]{:S(2)}) collective-permute-start(bf16[800,128]{1,0:T(8,128)(2,1)S(1)} %get-tuple-element.56), channel_id=1, source_target_pairs={{0,48},{1,49},{2,50},{3,51},{4,52},{5,53},{6,54},{7,55},{8,56},{9,... | collective-permute-start | bytes 614408 | tf_op jit(solution)/shard_map/ppermute | solution.py:476
  55.7 8.7 %collective-permute-start.14 = (bf16[800,128]{1,0:T(8,128)(2,1)S(1)}, bf16[800,128]{1,0:T(8,128)(2,1)S(1)}, u32[]{:S(2)}, u32[]{:S(2)}) collective-permute-start(bf16[800,128]{1,0:T(8,128)(2,1)S(1)} %sum_mid.1.own), channel_id=1, source_target_pairs={{0,12},{1,13},{2,14},{3,15},{4,0},{5,1},{6,2},{7,3},{8,4},{9,5},{1... | collective-permute-start | bytes 614408 | tf_op jit(solution)/shard_map/ppermute | solution.py:477
  59.5 6.2 %collective-permute-start.13 = (bf16[800,128]{1,0:T(8,128)(2,1)S(1)}, bf16[800,128]{1,0:T(8,128)(2,1)S(1)}, u32[]{:S(2)}, u32[]{:S(2)}) collective-permute-start(bf16[800,128]{1,0:T(8,128)(2,1)S(1)} %sum_mid.1.own), channel_id=1, source_target_pairs={{0,8},{1,9},{2,10},{3,11},{4,12},{5,13},{6,14},{7,15},{8,0},{9,1},... | collective-permute-start | bytes 614408 | tf_op jit(solution)/shard_map/ppermute | solution.py:477
  59.5 8.3 %collective-permute-start.12 = (bf16[800,128]{1,0:T(8,128)(2,1)S(1)}, bf16[800,128]{1,0:T(8,128)(2,1)S(1)}, u32[]{:S(2)}, u32[]{:S(2)}) collective-permute-start(bf16[800,128]{1,0:T(8,128)(2,1)S(1)} %sum_mid.1.own), channel_id=1, source_target_pairs={{0,4},{1,5},{2,6},{3,7},{4,8},{5,9},{6,10},{7,11},{8,12},{9,13},{1... | collective-permute-start | bytes 614408 | tf_op jit(solution)/shard_map/ppermute | solution.py:477
  67.9 7.3 %collective-permute-start.17 = (bf16[808,128]{1,0:T(8,128)(2,1)S(1)}, bf16[808,128]{1,0:T(8,128)(2,1)S(1)}, u32[]{:S(2)}, u32[]{:S(2)}) collective-permute-start(bf16[808,128]{1,0:T(8,128)(2,1)S(1)} %sum_cross.1), channel_id=1, source_target_pairs={{0,48},{1,49},{2,50},{3,51},{4,52},{5,53},{6,54},{7,55},{8,56},{9,... | collective-permute-start | bytes 620552 | tf_op jit(solution)/shard_map/ppermute | solution.py:478
  70.3 6.2 %collective-permute-start.16 = (bf16[808,128]{1,0:T(8,128)(2,1)S(1)}, bf16[808,128]{1,0:T(8,128)(2,1)S(1)}, u32[]{:S(2)}, u32[]{:S(2)}) collective-permute-start(bf16[808,128]{1,0:T(8,128)(2,1)S(1)} %sum_cross.1), channel_id=1, source_target_pairs={{0,32},{1,33},{2,34},{3,35},{4,36},{5,37},{6,38},{7,39},{8,40},{9,... | collective-permute-start | bytes 620552 | tf_op jit(solution)/shard_map/ppermute | solution.py:478
  71.1 7.8 %collective-permute-start.15 = (bf16[808,128]{1,0:T(8,128)(2,1)S(1)}, bf16[808,128]{1,0:T(8,128)(2,1)S(1)}, u32[]{:S(2)}, u32[]{:S(2)}) collective-permute-start(bf16[808,128]{1,0:T(8,128)(2,1)S(1)} %sum_cross.1), channel_id=1, source_target_pairs={{0,16},{1,17},{2,18},{3,19},{4,20},{5,21},{6,22},{7,23},{8,24},{9,... | collective-permute-start | bytes 620552 | tf_op jit(solution)/shard_map/ppermute | solution.py:478
  79.0 25.3 %collective-permute-start.20 = (bf16[4,808,128]{2,1,0:T(8,128)(2,1)S(1)}, bf16[4,808,128]{2,1,0:T(8,128)(2,1)S(1)}, u32[]{:S(2)}, u32[]{:S(2)}) collective-permute-start(bf16[4,808,128]{2,1,0:T(8,128)(2,1)S(1)} %pad_maximum_fusion.refs_0_), channel_id=1, source_target_pairs={{0,3},{1,0},{2,1},{3,2},{4,7},{5,4},{6,5},{7,6},{8,11},{9,8},{10,9... | collective-permute-start | bytes 2482184 | tf_op jit(solution)/shard_map/ppermute | solution.py:481
  81.5 22.9 %collective-permute-start.19 = (bf16[4,808,128]{2,1,0:T(8,128)(2,1)S(1)}, bf16[4,808,128]{2,1,0:T(8,128)(2,1)S(1)}, u32[]{:S(2)}, u32[]{:S(2)}) collective-permute-start(bf16[4,808,128]{2,1,0:T(8,128)(2,1)S(1)} %pad_maximum_fusion.refs_0_), channel_id=1, source_target_pairs={{0,2},{1,3},{2,0},{3,1},{4,6},{5,7},{6,4},{7,5},{8,10},{9,11},{10,... | collective-permute-start | bytes 2482184 | tf_op jit(solution)/shard_map/ppermute | solution.py:481
  81.8 22.6 %collective-permute-start.18 = (bf16[4,808,128]{2,1,0:T(8,128)(2,1)S(1)}, bf16[4,808,128]{2,1,0:T(8,128)(2,1)S(1)}, u32[]{:S(2)}, u32[]{:S(2)}) collective-permute-start(bf16[4,808,128]{2,1,0:T(8,128)(2,1)S(1)} %pad_maximum_fusion.refs_0_), channel_id=1, source_target_pairs={{0,1},{1,2},{2,3},{3,0},{4,5},{5,6},{6,7},{7,4},{8,9},{9,10},{10,1... | collective-permute-start | bytes 2482184 | tf_op jit(solution)/shard_map/ppermute | solution.py:481
  98.8 14.8 %collective-permute-start.21 = (bf16[4,808,128]{2,1,0:T(8,128)(2,1)S(1)}, bf16[4,808,128]{2,1,0:T(8,128)(2,1)S(1)}, u32[]{:S(2)}, u32[]{:S(2)}) collective-permute-start(bf16[4,808,128]{2,1,0:T(8,128)(2,1)S(1)} %pad_maximum_fusion.refs_0_), channel_id=1, source_target_pairs={{0,64},{64,0},{1,65},{65,1},{2,66},{66,2},{3,67},{67,3},{4,68},{68... | collective-permute-start | bytes 2482184 | tf_op jit(solution)/shard_map/ppermute | solution.py:485
  104.4 9.2 %collective-permute-start.22 = (bf16[4,808,128]{2,1,0:T(8,128)(2,1)S(1)}, bf16[4,808,128]{2,1,0:T(8,128)(2,1)S(1)}, u32[]{:S(2)}, u32[]{:S(2)}) collective-permute-start(bf16[4,808,128]{2,1,0:T(8,128)(2,1)S(1)} %collective-permute-done.18.refs_1_), channel_id=1, source_target_pairs={{0,64},{64,0},{1,65},{65,1},{2,66},{66,2},{3,67},{67,3},{4,68},{68... | collective-permute-start | bytes 2482184 | tf_op jit(solution)/shard_map/ppermute | solution.py:488
  108.8 4.8 %collective-permute-start.23 = (bf16[4,808,128]{2,1,0:T(8,128)(2,1)S(1)}, bf16[4,808,128]{2,1,0:T(8,128)(2,1)S(1)}, u32[]{:S(2)}, u32[]{:S(2)}) collective-permute-start(bf16[4,808,128]{2,1,0:T(8,128)(2,1)S(1)} %collective-permute-done.19.refs_2_), channel_id=1, source_target_pairs={{0,64},{64,0},{1,65},{65,1},{2,66},{66,2},{3,67},{67,3},{4,68},{68... | collective-permute-start | bytes 2482184 | tf_op jit(solution)/shard_map/ppermute | solution.py:488
  108.8 4.8 %collective-permute-start.24 = (bf16[4,808,128]{2,1,0:T(8,128)(2,1)S(1)}, bf16[4,808,128]{2,1,0:T(8,128)(2,1)S(1)}, u32[]{:S(2)}, u32[]{:S(2)}) collective-permute-start(bf16[4,808,128]{2,1,0:T(8,128)(2,1)S(1)} %collective-permute-done.20.refs_3_), channel_id=1, source_target_pairs={{0,64},{64,0},{1,65},{65,1},{2,66},{66,2},{3,67},{67,3},{4,68},{68... | collective-permute-start | bytes 2482184 | tf_op jit(solution)/shard_map/ppermute | solution.py:488
  109.4 4.2 %collective-permute-start.25 = (bf16[2,50,1280]{2,1,0:T(8,128)(2,1)S(1)}, bf16[2,50,1280]{2,1,0:T(8,128)(2,1)S(1)}, u32[]{:S(2)}, u32[]{:S(2)}) collective-permute-start(bf16[2,50,1280]{2,1,0:T(8,128)(2,1)S(1)} %get-tuple-element.69), channel_id=1, source_target_pairs={{64,0},{65,1},{66,2},{67,3},{68,4},{69,5},{70,6},{71,7},{72,8},{73... | collective-permute-start | bytes 768008 | tf_op jit(solution)/shard_map/ppermute | solution.py:484
